TPU v7x, 32 devices: a whole 2x2x4 slice. The times are simulated.
32 devices in a mesh: replica: 8 (over y, x, core), shard: 4 (over z).
Axes of the slice: x: 2, y: 2, z: 4, core: 2. Of those that a mesh axis runs over, the one named last changes fastest.
Arguments:
- layer_input: bfloat16 [64, 512, 768], P(('replica', 'shard')), may hold values from -6 to 6
- out_grad: bfloat16 [64, 512, 768], P(('replica', 'shard')), may hold values from -6 to 6
- seq_lengths: int32 [64], replicated, may hold values from 64 to 512, as said below
- deal_order: int32 [64], replicated, may hold values from 0 to 63, as said below
- w_query: bfloat16 [768, 768], P('shard'), may hold values from -0.21875 to 0.21875
- b_query: bfloat16 [768], P('shard'), may hold values from -1.75 to 1.75
- w_key: bfloat16 [768, 768], P('shard'), may hold values from -0.21875 to 0.21875
- w_value: bfloat16 [768, 768], P('shard'), may hold values from -0.21875 to 0.21875
- b_value: bfloat16 [768], P('shard'), may hold values from -0.0625 to 0.0625
- w_output: bfloat16 [768, 768], P('shard'), may hold values from -4 to 4
- b_output: bfloat16 [768], P('shard'), may hold values from -1.25 to 1.25
- first_gain: bfloat16 [768], P('shard'), may hold values from 0.099609375 to 1.8984375
- first_shift: bfloat16 [768], P('shard'), may hold values from -1.75 to 1.75
- w_inner: bfloat16 [768, 3072], P('shard'), may hold values from -0.21875 to 0.21875
- b_inner: bfloat16 [3072], P('shard'), may hold values from -1.75 to 1.75
- w_outer: bfloat16 [3072, 768], P('shard'), may hold values from -0.109375 to 0.109375
- b_outer: bfloat16 [768], P('shard'), may hold values from -1.75 to 1.75
- second_gain: bfloat16 [768], P('shard'), may hold values from 0.099609375 to 1.8984375
- second_shift: bfloat16 [768], P('shard'), may hold values from -1.75 to 1.75
Outputs:
- layer_output: bfloat16 [64, 512, 768], P(('replica', 'shard'))
- input_grad: bfloat16 [64, 512, 768], P(('replica', 'shard'))
- grad_wquery: float32 [768, 768], P('shard')
- grad_bquery: float32 [768], P('shard')
- grad_wkey: float32 [768, 768], P('shard')
- grad_wvalue: float32 [768, 768], P('shard')
- grad_bvalue: float32 [768], P('shard')
- grad_woutput: float32 [768, 768], P('shard')
- grad_boutput: float32 [768], P('shard')
- grad_firstgain: float32 [768], P('shard')
- grad_firstshift: float32 [768], P('shard')
- grad_winner: float32 [768, 3072], P('shard')
- grad_binner: float32 [3072], P('shard')
- grad_wouter: float32 [3072, 768], P('shard')
- grad_bouter: float32 [768], P('shard')
- grad_secondgain: float32 [768], P('shard')
- grad_secondshift: float32 [768], P('shard')
Inputs may be any that keep to these rules, and one draw needn't show every extreme that they name: `seq_lengths`: every length is at least 64; the two sequences placed in slots 2 j and 2 j + 1 have lengths that sum to at most 576; some sequence has exactly 512. A permutation of the 64 sequences: slot i receives sequence deal_order[i] of the given order.
All inputs are finite; a program needn't handle non-finite values.
Results may differ from a plain program's by a relative error of at most 0.02.
Values may be sent and summed in bfloat16 or wider, within the bound.
No kernel may reach another device: no remote copies, remote signals or barrier semaphores. Data moves between devices by JAX's collectives and lax.ppermute only.
A program may use at most 128 MiB of HBM per device.

v0:
```python
import math

import jax
import jax.numpy as jnp
from jax import lax
from jax.sharding import PartitionSpec as P

HEADS = 12
MAXLEN = 512
MINLEN = 64


NORM_EPS = 1e-12
SCORE_SCALE = 0.125
MASK_VALUE = -1e30


def dot_rows(left_op, right_op):
    return jnp.dot(left_op, right_op, preferred_element_type=jnp.float32)


def dot_left(left_op, right_op):
    return lax.dot_general(
        left_op, right_op, (((0,), (0,)), ((), ())), preferred_element_type=jnp.float32
    )


def dot_right(left_op, right_op):
    return lax.dot_general(
        left_op, right_op, (((1,), (1,)), ((), ())), preferred_element_type=jnp.float32
    )


def normalize(values, gain_vec, shift_vec):
    center = values - jnp.mean(values, axis=-1, keepdims=True)
    inverse = lax.rsqrt(jnp.mean(center * center, axis=-1, keepdims=True) + NORM_EPS)
    normed = center * inverse
    return (normed * gain_vec + shift_vec, normed, inverse)


def normalize_back(upstream, normed, inverse, gain_vec):
    scaled = upstream * gain_vec
    centered = (
        scaled
        - jnp.mean(scaled, axis=-1, keepdims=True)
        - normed * jnp.mean(scaled * normed, axis=-1, keepdims=True)
    )
    return (inverse * centered, jnp.sum(upstream * normed, axis=0), jnp.sum(upstream, axis=0))


def gelu_exact(values):
    return 0.5 * values * (1.0 + lax.erf(values * (1.0 / math.sqrt(2.0))))


def gelu_slope(values):
    cumulative = 0.5 * (1.0 + lax.erf(values * (1.0 / math.sqrt(2.0))))
    density = jnp.exp(-0.5 * values * values) * (1.0 / math.sqrt(2.0 * math.pi))
    return cumulative + values * density


def pack_pair(leading, trailing, lead_len, trail_len, capacity):
    seq_rows = leading.shape[0]
    features = leading.shape[1]
    row_ids = jnp.arange(seq_rows, dtype=jnp.int32)[:, None]
    leading = jnp.where(row_ids < lead_len, leading, jnp.zeros_like(leading))
    trailing = jnp.where(row_ids < trail_len, trailing, jnp.zeros_like(trailing))
    head_part = jnp.concatenate(
        [leading, jnp.zeros((capacity - seq_rows, features), leading.dtype)], axis=0
    )
    padded = jnp.concatenate(
        [
            jnp.zeros((capacity, features), leading.dtype),
            trailing,
            jnp.zeros((capacity - seq_rows, features), leading.dtype),
        ],
        axis=0,
    )
    tail_part = lax.dynamic_slice_in_dim(padded, capacity - lead_len, capacity, 0)
    return head_part + tail_part


def unpack_pair(packed, lead_len, trail_len, seq_rows):
    features = packed.shape[1]
    row_ids = jnp.arange(seq_rows, dtype=jnp.int32)[:, None]
    leading = jnp.where(
        row_ids < lead_len, packed[:seq_rows], jnp.zeros((seq_rows, features), packed.dtype)
    )
    extended = jnp.concatenate([packed, jnp.zeros((seq_rows, features), packed.dtype)], axis=0)
    trailing = lax.dynamic_slice_in_dim(extended, lead_len, seq_rows, 0)
    trailing = jnp.where(row_ids < trail_len, trailing, jnp.zeros_like(trailing))
    return jnp.stack([leading, trailing], axis=0)


def on_device(
    layer_input,
    out_grad,
    seq_lengths,
    deal_order,
    w_query,
    b_query,
    w_key,
    w_value,
    b_value,
    w_output,
    b_output,
    first_gain,
    first_shift,
    w_inner,
    b_inner,
    w_outer,
    b_outer,
    second_gain,
    second_shift,
):
    devices = lax.axis_size("replica") * lax.axis_size("shard")
    device_pos = lax.axis_index("replica") * lax.axis_size("shard") + lax.axis_index("shard")
    seq_rows = layer_input.shape[1]
    features = layer_input.shape[2]
    piece_rows = seq_rows // devices
    head_size = features // HEADS
    capacity = MAXLEN + MINLEN
    given_in, given_cot = (
        lax.all_to_all(
            layer_input.reshape(2, devices, piece_rows, features),
            ("replica", "shard"),
            split_axis=1,
            concat_axis=0,
            tiled=True,
        ),
        lax.all_to_all(
            out_grad.reshape(2, devices, piece_rows, features),
            ("replica", "shard"),
            split_axis=1,
            concat_axis=0,
            tiled=True,
        ),
    )
    chosen_in = jnp.take(given_in, deal_order, axis=0)
    chosen_cot = jnp.take(given_cot, deal_order, axis=0)
    slot_in, slot_cot = (
        lax.all_to_all(chosen_in, ("replica", "shard"), split_axis=0, concat_axis=1, tiled=True),
        lax.all_to_all(chosen_cot, ("replica", "shard"), split_axis=0, concat_axis=1, tiled=True),
    )
    slot_in = slot_in.reshape(2, seq_rows, features)
    slot_cot = slot_cot.reshape(2, seq_rows, features)
    my_slots = lax.dynamic_slice_in_dim(deal_order, device_pos * 2, 2, 0)
    slot_lengths = jnp.take(seq_lengths, my_slots, axis=0)
    lead_len = slot_lengths[0]
    trail_len = slot_lengths[1]
    packed_in = pack_pair(slot_in[0], slot_in[1], lead_len, trail_len, capacity)
    packed_cot = pack_pair(slot_cot[0], slot_cot[1], lead_len, trail_len, capacity)
    key_valid = jnp.arange(capacity, dtype=jnp.int32) < lead_len + trail_len
    attn_full = (
        lax.all_gather(w_query, "shard", axis=0, tiled=True),
        lax.all_gather(b_query, "shard", axis=0, tiled=True),
        lax.all_gather(w_key, "shard", axis=0, tiled=True),
        lax.all_gather(w_value, "shard", axis=0, tiled=True),
        lax.all_gather(b_value, "shard", axis=0, tiled=True),
        lax.all_gather(w_output, "shard", axis=0, tiled=True),
        lax.all_gather(b_output, "shard", axis=0, tiled=True),
        lax.all_gather(first_gain, "shard", axis=0, tiled=True),
        lax.all_gather(first_shift, "shard", axis=0, tiled=True),
    )
    wq_full, bq_full, wk_full, wv_full, bv_full, wo_full, bo_full, gain_one, shift_one = attn_full
    query_low = (dot_rows(packed_in, wq_full) + bq_full.astype(jnp.float32)).astype(jnp.bfloat16)
    key_low = dot_rows(packed_in, wk_full).astype(jnp.bfloat16)
    value_low = (dot_rows(packed_in, wv_full) + bv_full.astype(jnp.float32)).astype(jnp.bfloat16)

    def head_forward(head_index):
        offset = head_index * head_size
        query_head = lax.dynamic_slice_in_dim(query_low, offset, head_size, 1)
        key_head = lax.dynamic_slice_in_dim(key_low, offset, head_size, 1)
        value_head = lax.dynamic_slice_in_dim(value_low, offset, head_size, 1)
        scores = jnp.where(
            key_valid[None, :], dot_right(query_head, key_head) * SCORE_SCALE, MASK_VALUE
        )
        row_max = jnp.max(scores, axis=1, keepdims=True)
        log_total = row_max + jnp.log(jnp.sum(jnp.exp(scores - row_max), axis=1, keepdims=True))
        attn_probs = jnp.exp(scores - log_total)
        return (dot_rows(attn_probs.astype(jnp.bfloat16), value_head), log_total[:, 0])

    head_mix, log_totals = lax.map(head_forward, jnp.arange(HEADS, dtype=jnp.int32))
    mix_low = jnp.transpose(head_mix, (1, 0, 2)).reshape(capacity, features).astype(jnp.bfloat16)
    branch = dot_rows(mix_low, wo_full) + bo_full.astype(jnp.float32)
    first_out, normed_one, inverse_one = normalize(
        packed_in.astype(jnp.float32) + branch,
        gain_one.astype(jnp.float32),
        shift_one.astype(jnp.float32),
    )
    ffn_full = (
        lax.all_gather(w_inner, "shard", axis=0, tiled=True),
        lax.all_gather(b_inner, "shard", axis=0, tiled=True),
        lax.all_gather(w_outer, "shard", axis=0, tiled=True),
        lax.all_gather(b_outer, "shard", axis=0, tiled=True),
        lax.all_gather(second_gain, "shard", axis=0, tiled=True),
        lax.all_gather(second_shift, "shard", axis=0, tiled=True),
    )
    wi_full, bi_full, wout_full, bout_full, gain_two, shift_two = ffn_full
    hidden_low = first_out.astype(jnp.bfloat16)
    inner_pre = dot_rows(hidden_low, wi_full) + bi_full.astype(jnp.float32)
    act_low = gelu_exact(inner_pre).astype(jnp.bfloat16)
    outer_out = dot_rows(act_low, wout_full) + bout_full.astype(jnp.float32)
    packed_out, normed_two, inverse_two = normalize(
        first_out + outer_out, gain_two.astype(jnp.float32), shift_two.astype(jnp.float32)
    )
    back_ffn = (
        lax.all_gather(w_inner, "shard", axis=0, tiled=True),
        lax.all_gather(b_inner, "shard", axis=0, tiled=True),
        lax.all_gather(w_outer, "shard", axis=0, tiled=True),
        lax.all_gather(b_outer, "shard", axis=0, tiled=True),
        lax.all_gather(second_gain, "shard", axis=0, tiled=True),
        lax.all_gather(second_shift, "shard", axis=0, tiled=True),
    )
    wi_back = back_ffn[0]
    wout_back = back_ffn[2]
    gain_back_two = back_ffn[4]
    second_back, grad_secondgain, grad_secondshift = normalize_back(
        packed_cot.astype(jnp.float32), normed_two, inverse_two, gain_back_two.astype(jnp.float32)
    )
    outer_grad = second_back.astype(jnp.bfloat16)
    grad_bouter = jnp.sum(outer_grad.astype(jnp.float32), axis=0)
    grad_wouter = dot_left(act_low, outer_grad)
    inner_grad = (dot_right(outer_grad, wout_back) * gelu_slope(inner_pre)).astype(jnp.bfloat16)
    grad_binner = jnp.sum(inner_grad.astype(jnp.float32), axis=0)
    grad_winner = dot_left(hidden_low, inner_grad)
    first_total = second_back + dot_right(inner_grad, wi_back)
    back_attn = (
        lax.all_gather(w_query, "shard", axis=0, tiled=True),
        lax.all_gather(b_query, "shard", axis=0, tiled=True),
        lax.all_gather(w_key, "shard", axis=0, tiled=True),
        lax.all_gather(w_value, "shard", axis=0, tiled=True),
        lax.all_gather(b_value, "shard", axis=0, tiled=True),
        lax.all_gather(w_output, "shard", axis=0, tiled=True),
        lax.all_gather(b_output, "shard", axis=0, tiled=True),
        lax.all_gather(first_gain, "shard", axis=0, tiled=True),
        lax.all_gather(first_shift, "shard", axis=0, tiled=True),
    )
    wq_back = back_attn[0]
    wk_back = back_attn[2]
    wv_back = back_attn[3]
    wo_back = back_attn[5]
    gain_back_one = back_attn[7]
    first_back, grad_firstgain, grad_firstshift = normalize_back(
        first_total, normed_one, inverse_one, gain_back_one.astype(jnp.float32)
    )
    branch_grad = first_back.astype(jnp.bfloat16)
    grad_boutput = jnp.sum(branch_grad.astype(jnp.float32), axis=0)
    grad_woutput = dot_left(mix_low, branch_grad)
    mix_grad = dot_right(branch_grad, wo_back).astype(jnp.bfloat16)

    def head_backward(head_index):
        offset = head_index * head_size
        query_head = lax.dynamic_slice_in_dim(query_low, offset, head_size, 1)
        key_head = lax.dynamic_slice_in_dim(key_low, offset, head_size, 1)
        value_head = lax.dynamic_slice_in_dim(value_low, offset, head_size, 1)
        mix_head_grad = lax.dynamic_slice_in_dim(mix_grad, offset, head_size, 1)
        log_total = lax.dynamic_index_in_dim(log_totals, head_index, 0, keepdims=False)
        scores = jnp.where(
            key_valid[None, :], dot_right(query_head, key_head) * SCORE_SCALE, MASK_VALUE
        )
        attn_probs = jnp.exp(scores - log_total[:, None])
        prob_grad = dot_right(mix_head_grad, value_head)
        value_head_grad = dot_left(attn_probs.astype(jnp.bfloat16), mix_head_grad)
        row_dot = jnp.sum(attn_probs * prob_grad, axis=1, keepdims=True)
        score_grad = (attn_probs * (prob_grad - row_dot)).astype(jnp.bfloat16)
        query_head_grad = dot_rows(score_grad, key_head) * SCORE_SCALE
        key_head_grad = dot_left(score_grad, query_head) * SCORE_SCALE
        return (query_head_grad, key_head_grad, value_head_grad)

    query_heads, key_heads, value_heads = lax.map(head_backward, jnp.arange(HEADS, dtype=jnp.int32))
    query_grad = (
        jnp.transpose(query_heads, (1, 0, 2)).reshape(capacity, features).astype(jnp.bfloat16)
    )
    key_grad = jnp.transpose(key_heads, (1, 0, 2)).reshape(capacity, features).astype(jnp.bfloat16)
    value_grad = (
        jnp.transpose(value_heads, (1, 0, 2)).reshape(capacity, features).astype(jnp.bfloat16)
    )
    grad_bquery = jnp.sum(query_grad.astype(jnp.float32), axis=0)
    grad_bvalue = jnp.sum(value_grad.astype(jnp.float32), axis=0)
    grad_wquery = dot_left(packed_in, query_grad)
    grad_wkey = dot_left(packed_in, key_grad)
    grad_wvalue = dot_left(packed_in, value_grad)
    input_packed = (
        first_back
        + dot_right(query_grad, wq_back)
        + dot_right(key_grad, wk_back)
        + dot_right(value_grad, wv_back)
    )
    layer_slots = unpack_pair(packed_out, lead_len, trail_len, seq_rows).astype(jnp.bfloat16)
    input_slots = unpack_pair(input_packed, lead_len, trail_len, seq_rows).astype(jnp.bfloat16)
    inverse_order = jnp.argsort(deal_order)
    slot_out, slot_back = (
        lax.all_to_all(
            layer_slots.reshape(2, devices, piece_rows, features),
            ("replica", "shard"),
            split_axis=1,
            concat_axis=0,
            tiled=True,
        ),
        lax.all_to_all(
            input_slots.reshape(2, devices, piece_rows, features),
            ("replica", "shard"),
            split_axis=1,
            concat_axis=0,
            tiled=True,
        ),
    )
    given_out = jnp.take(slot_out, inverse_order, axis=0)
    given_back = jnp.take(slot_back, inverse_order, axis=0)
    final_out, final_back = (
        lax.all_to_all(given_out, ("replica", "shard"), split_axis=0, concat_axis=1, tiled=True),
        lax.all_to_all(given_back, ("replica", "shard"), split_axis=0, concat_axis=1, tiled=True),
    )
    final_out = final_out.reshape(2, seq_rows, features)
    final_back = final_back.reshape(2, seq_rows, features)
    all_parts = (
        lax.psum_scatter(
            grad_wquery.astype(jnp.bfloat16), "shard", scatter_dimension=0, tiled=True
        ).astype(jnp.float32),
        lax.psum_scatter(
            grad_bquery.astype(jnp.bfloat16), "shard", scatter_dimension=0, tiled=True
        ).astype(jnp.float32),
        lax.psum_scatter(
            grad_wkey.astype(jnp.bfloat16), "shard", scatter_dimension=0, tiled=True
        ).astype(jnp.float32),
        lax.psum_scatter(
            grad_wvalue.astype(jnp.bfloat16), "shard", scatter_dimension=0, tiled=True
        ).astype(jnp.float32),
        lax.psum_scatter(
            grad_bvalue.astype(jnp.bfloat16), "shard", scatter_dimension=0, tiled=True
        ).astype(jnp.float32),
        lax.psum_scatter(
            grad_woutput.astype(jnp.bfloat16), "shard", scatter_dimension=0, tiled=True
        ).astype(jnp.float32),
        lax.psum_scatter(
            grad_boutput.astype(jnp.bfloat16), "shard", scatter_dimension=0, tiled=True
        ).astype(jnp.float32),
        lax.psum_scatter(
            grad_firstgain.astype(jnp.bfloat16), "shard", scatter_dimension=0, tiled=True
        ).astype(jnp.float32),
        lax.psum_scatter(
            grad_firstshift.astype(jnp.bfloat16), "shard", scatter_dimension=0, tiled=True
        ).astype(jnp.float32),
        lax.psum_scatter(
            grad_winner.astype(jnp.bfloat16), "shard", scatter_dimension=0, tiled=True
        ).astype(jnp.float32),
        lax.psum_scatter(
            grad_binner.astype(jnp.bfloat16), "shard", scatter_dimension=0, tiled=True
        ).astype(jnp.float32),
        lax.psum_scatter(
            grad_wouter.astype(jnp.bfloat16), "shard", scatter_dimension=0, tiled=True
        ).astype(jnp.float32),
        lax.psum_scatter(
            grad_bouter.astype(jnp.bfloat16), "shard", scatter_dimension=0, tiled=True
        ).astype(jnp.float32),
        lax.psum_scatter(
            grad_secondgain.astype(jnp.bfloat16), "shard", scatter_dimension=0, tiled=True
        ).astype(jnp.float32),
        lax.psum_scatter(
            grad_secondshift.astype(jnp.bfloat16), "shard", scatter_dimension=0, tiled=True
        ).astype(jnp.float32),
    )
    grad_sums = (
        lax.psum(all_parts[0].astype(jnp.bfloat16), "replica").astype(jnp.float32),
        lax.psum(all_parts[1].astype(jnp.bfloat16), "replica").astype(jnp.float32),
        lax.psum(all_parts[2].astype(jnp.bfloat16), "replica").astype(jnp.float32),
        lax.psum(all_parts[3].astype(jnp.bfloat16), "replica").astype(jnp.float32),
        lax.psum(all_parts[4].astype(jnp.bfloat16), "replica").astype(jnp.float32),
        lax.psum(all_parts[5].astype(jnp.bfloat16), "replica").astype(jnp.float32),
        lax.psum(all_parts[6].astype(jnp.bfloat16), "replica").astype(jnp.float32),
        lax.psum(all_parts[7].astype(jnp.bfloat16), "replica").astype(jnp.float32),
        lax.psum(all_parts[8].astype(jnp.bfloat16), "replica").astype(jnp.float32),
        lax.psum(all_parts[9].astype(jnp.bfloat16), "replica").astype(jnp.float32),
        lax.psum(all_parts[10].astype(jnp.bfloat16), "replica").astype(jnp.float32),
        lax.psum(all_parts[11].astype(jnp.bfloat16), "replica").astype(jnp.float32),
        lax.psum(all_parts[12].astype(jnp.bfloat16), "replica").astype(jnp.float32),
        lax.psum(all_parts[13].astype(jnp.bfloat16), "replica").astype(jnp.float32),
        lax.psum(all_parts[14].astype(jnp.bfloat16), "replica").astype(jnp.float32),
    )
    return (
        final_out,
        final_back,
        grad_sums[0],
        grad_sums[1],
        grad_sums[2],
        grad_sums[3],
        grad_sums[4],
        grad_sums[5],
        grad_sums[6],
        grad_sums[7],
        grad_sums[8],
        grad_sums[9],
        grad_sums[10],
        grad_sums[11],
        grad_sums[12],
        grad_sums[13],
        grad_sums[14],
    )


def solution(mesh):
    in_specs = (
        P(("replica", "shard"), None, None),
        P(("replica", "shard"), None, None),
        P(),
        P(),
        P("shard", None),
        P("shard"),
        P("shard", None),
        P("shard", None),
        P("shard"),
        P("shard", None),
        P("shard"),
        P("shard"),
        P("shard"),
        P("shard", None),
        P("shard"),
        P("shard", None),
        P("shard"),
        P("shard"),
        P("shard"),
    )
    out_specs = (
        P(("replica", "shard"), None, None),
        P(("replica", "shard"), None, None),
        P("shard", None),
        P("shard"),
        P("shard", None),
        P("shard", None),
        P("shard"),
        P("shard", None),
        P("shard"),
        P("shard"),
        P("shard"),
        P("shard", None),
        P("shard"),
        P("shard", None),
        P("shard"),
        P("shard"),
        P("shard"),
    )
    return jax.shard_map(
        on_device, mesh=mesh, in_specs=in_specs, out_specs=out_specs, check_vma=False
    )
```

profile of v0, /device:TPU:0, one launch (start us, length us, event | category | flops | bytes accessed | tf_op | source)
XLA Modules:
  0.0 1093.3 jit_solution(2699670565839886225)
XLA Ops:
  11.5 7.3 all-to-all-start
  21.5 52.1 %all-to-all-done = bf16[2,32,16,768]{3,2,0,1:T(8,128)(2,1)S(1)} async-done(((bf16[2,32,16,768]{3,2,0,1:T(8,128)(2,1)}), bf16[2,32,16,768]{3,2,0,1:T(8,128)(2,1)S(1)}, u32[]{:S(2)}, u32[]{:S(2)}) %all-to-all-start) | async-done | bytes 1572896 | tf_op jit(solution)/shard_map/all_to_all | solution.py:123
  73.6 4.7 all-to-all-start.4
  80.7 51.6 %all-to-all-done.4 = bf16[2,32,16,768]{3,2,0,1:T(8,128)(2,1)S(1)} async-done(((bf16[2,32,16,768]{3,2,0,1:T(8,128)(2,1)}), bf16[2,32,16,768]{3,2,0,1:T(8,128)(2,1)S(1)}, u32[]{:S(2)}, u32[]{:S(2)}) %all-to-all-start.4) | async-done | bytes 1572896 | tf_op jit(solution)/shard_map/all_to_all | solution.py:130
  137.1 63.2 %all_to_all.132 = bf16[64,1,16,768]{3,2,1,0:T(8,128)(2,1)S(1)} all-to-all(bf16[64,1,16,768]{3,2,1,0:T(8,128)(2,1)S(1)} %get-tuple-element.277), channel_id=1, replica_groups=mesh['replica'=8,'shard'=4] {'replica','shard'}, dimensions={0} | all-to-all | bytes 3145728 | tf_op jit(solution)/shard_map/all_to_all | solution.py:142
  200.4 4.2 all-to-all-start.1
  210.9 79.1 %all-reduce.24 = (bf16[768]{0:T(1024)(128)(2,1)S(1)}, bf16[768]{0:T(1024)(128)(2,1)S(1)}, bf16[768]{0:T(1024)(128)(2,1)S(1)}, bf16[768]{0:T(1024)(128)(2,1)S(1)}...) all-reduce(bf16[768]{0:T(1024)(128)(2,1)S(1)} %dynamic-update-slice, ...), channel_id=1, replica_groups=mesh['replica'=8,'shard'=4] {'shard'}, use_global_device_ids=true, to_apply=%add.4 | all-reduce | flops 5376 | bytes 21504
  293.1 13.6 %all-gather = bf16[4,1,768]{2,1,0:T(2,128)(2,1)S(1)} all-gather(bf16[1,1,768]{2,1,0:T(2,128)(2,1)S(1)} %reshape.275), channel_id=1, replica_groups=mesh['replica'=8,'shard'=4] {'shard'}, dimensions={0}, use_global_device_ids=true | all-gather | bytes 7680 | tf_op jit(solution)/shard_map/all_gather | solution.py:192
  322.8 60.5 %while.28 = (s32[]{:T(128)}, bf16[12,576,64]{1,2,0:T(8,128)(2,1)}, f32[12,576]{1,0:T(8,128)}, s32[12]{0:T(128)}, bf16[576,768]{1,0:T(8,128)(2,1)S(1)}, /*index=5...) while((s32[]{:T(128)}, bf16[12,576,64]{1,2,0:T(8,128)(2,1)}, ...), condition=%wide.region_3.5_spmd.clone, body=%wide.region_0.4_spmd.clone.sunk | while | flops 87257088 | bytes 4765435 | solution.py:182
  388.7 8.0 multiply_convert_fusion.1
  396.7 13.0 %all-gather.18.cloned.1.call-done = bf16[3072,768]{1,0:T(8,128)(2,1)} async-done(((bf16[768,768]{1,0:T(8,128)(2,1)}), bf16[3072,768]{1,0:T(8,128)(2,1)}) %all-gather.18.cloned.1.call-update) | async-done | bytes 4718608 | tf_op jit(solution)/shard_map/all_gather | solution.py:193
  409.6 7.1 fusion.76
  419.8 6.3 fusion.77
  426.1 4.0 multiply_reduce_fusion.1
  436.4 159.4 %while.29 = (s32[]{:T(128)}, bf16[12,576,64]{1,2,0:T(8,128)(2,1)}, bf16[12,576,64]{1,2,0:T(8,128)(2,1)}, bf16[12,576,64]{1,2,0:T(8,128)(2,1)}, s32[12]{0:T(128)S...) while((s32[]{:T(128)}, bf16[12,576,64]{1,2,0:T(8,128)(2,1)}, ...), condition=%wide.region_15.17_spmd.clone, body=%wide.region_13.16_spmd.clone.sunk | while | flops 215396352 | bytes 18571892 | solution.py:270
  595.9 3.7 convolution_convert_fusion.3
  603.1 3.8 convolution_convert_fusion.4
  607.0 4.0 convolution_convert_fusion.2
  611.1 8.2 convolution_convert_fusion.1
  623.5 16.0 %all-reduce.23 = (bf16[768]{0:T(1024)(128)(2,1)S(1)}, bf16[768]{0:T(1024)(128)(2,1)S(1)}, bf16[768]{0:T(1024)(128)(2,1)S(1)}, bf16[768]{0:T(1024)(128)(2,1)S(1)}...) all-reduce(bf16[768]{0:T(1024)(128)(2,1)S(1)} %dynamic-update-slice, ...), channel_id=1, replica_groups=mesh['replica'=8,'shard'=4] {'shard'}, use_global_device_ids=true, to_apply=%add.11 | all-reduce | flops 9984 | bytes 39936
  647.8 4.0 all-to-all-start.2
  651.8 8.6 convolution_convert_fusion
  661.8 46.3 %all-to-all-done.2 = bf16[2,32,16,768]{3,2,0,1:T(8,128)(2,1)S(1)} async-done(((bf16[2,32,16,768]{3,2,0,1:T(8,128)(2,1)}), bf16[2,32,16,768]{3,2,0,1:T(8,128)(2,1)S(1)}, u32[]{:S(2)}, u32[]{:S(2)}) %all-to-all-start.2) | async-done | bytes 1572896 | tf_op jit(solution)/shard_map/all_to_all | solution.py:293
  708.0 3.8 all-to-all-start.6
  715.7 50.9 %all-to-all-done.6 = bf16[2,32,16,768]{3,2,0,1:T(8,128)(2,1)S(1)} async-done(((bf16[2,32,16,768]{3,2,0,1:T(8,128)(2,1)}), bf16[2,32,16,768]{3,2,0,1:T(8,128)(2,1)S(1)}, u32[]{:S(2)}, u32[]{:S(2)}) %all-to-all-start.6) | async-done | bytes 1572896 | tf_op jit(solution)/shard_map/all_to_all | solution.py:300
  768.4 3.4 fusion.49
  771.8 83.0 %all_to_all.133 = bf16[64,1,16,768]{3,2,1,0:T(8,128)(2,1)S(1)} all-to-all(bf16[64,1,16,768]{3,2,1,0:T(8,128)(2,1)S(1)} %get-tuple-element.272), channel_id=1, replica_groups=mesh['replica'=8,'shard'=4] {'replica','shard'}, dimensions={0} | all-to-all | bytes 3145728 | tf_op jit(solution)/shard_map/all_to_all | solution.py:311
  854.8 4.4 all-to-all-start.7
  859.3 30.1 %reduce-scatter.15.cloned.1.call-done = bf16[192,3072]{1,0:T(8,128)(2,1)} async-done(((bf16[768,3072]{1,0:T(8,128)(2,1)}), bf16[192,3072]{1,0:T(8,128)(2,1)}) %reduce-scatter.15.cloned.1.call-update) | async-done | bytes 1179664 | tf_op jit(solution)/shard_map/reduce_scatter | solution.py:344
  889.4 110.1 %reduce-scatter.17.cloned.1.call-done = bf16[768,768]{1,0:T(8,128)(2,1)} async-done(((bf16[3072,768]{1,0:T(8,128)(2,1)}), bf16[768,768]{1,0:T(8,128)(2,1)}) %reduce-scatter.17.cloned.1.call-update) | async-done | bytes 1179664 | tf_op jit(solution)/shard_map/reduce_scatter | solution.py:350
  1001.5 14.4 %all-reduce.21 = (bf16[192]{0:T(256)(128)(2,1)S(1)}, bf16[192]{0:T(256)(128)(2,1)S(1)}, bf16[192]{0:T(256)(128)(2,1)S(1)}, bf16[192]{0:T(256)(128)(2,1)S(1)}, bf...) all-reduce(bf16[192]{0:T(256)(128)(2,1)S(1)} %dynamic-slice.9, ...), channel_id=1, replica_groups=mesh['replica'=8,'shard'=4] {'replica'}, use_global_device_ids=true, to_apply=%region_20.22 | all-reduce | flops 2304 | bytes 9216 | tf_op jit(solution)/shard_map/psum | solution.py:365
  1023.6 54.6 %all-reduce.27.cloned.1.call-done = (bf16[192,768]{1,0:T(8,128)(2,1)}, bf16[192,768]{1,0:T(8,128)(2,1)}, bf16[192,768]{1,0:T(8,128)(2,1)}, bf16[192,768]{1,0:T(8...) async-done(((bf16[192,768]{1,0:T(8,128)(2,1)}, bf16[192,768]{1,0:T(8,128)(2,1)}, bf16[192,768]{1,0:T(8,128)(2,1)}, bf16[192,768]{1,0:T(8,128)(2,1)}, ...) | async-done | bytes 3538960 | tf_op jit(solution)/shard_map/psum | solution.py:364
  (587 shorter events, 267.9 us)
Async XLA Ops:
  7.2 198.2 %copy-start = (s32[64]{0:T(128)S(1)}, s32[64]{0:T(128)}, u32[]{:S(2)}) copy-start(s32[64]{0:T(128)} %param.27) | copy-start | bytes 772
  7.2 307.0 %all-gather.10.cloned.1.call-start = ((), (), s32[]{:S(2)}) async-start(), calls=%async_computation.15 | async-start | bytes 1474560 | tf_op jit(solution)/shard_map/all_gather | solution.py:156
  7.9 308.7 %all-gather.12.cloned.1.call-start = ((), (), s32[]{:S(2)}) async-start(), calls=%async_computation.16 | async-start | bytes 1474560 | tf_op jit(solution)/shard_map/all_gather | solution.py:157
  11.5 62.1 %all-to-all-start = ((bf16[2,32,16,768]{3,2,0,1:T(8,128)(2,1)}), bf16[2,32,16,768]{3,2,0,1:T(8,128)(2,1)S(1)}, u32[]{:S(2)}, u32[]{:S(2)}) async-start(bf16[2,32,16,768]{3,2,0,1:T(8,128)(2,1)} %copy.48), calls=%async_computation | async-start | bytes 3145728 | tf_op jit(solution)/shard_map/all_to_all | solution.py:123
  18.8 300.1 %all-gather.8.cloned.1.call-start = ((), (), s32[]{:S(2)}) async-start(), calls=%async_computation.14 | async-start | bytes 1474560 | tf_op jit(solution)/shard_map/all_gather | solution.py:154
  19.5 363.8 %all-gather.14.cloned.1.call-start = ((), (), s32[]{:S(2)}) async-start(), calls=%async_computation.17 | async-start | bytes 1474560 | tf_op jit(solution)/shard_map/all_gather | solution.py:159
  21.5 57.4 %copy-start.49 = (s32[64]{0:T(128)S(1)}, s32[64]{0:T(128)}, u32[]{:S(2)}) copy-start(s32[64]{0:T(128)} %param.28) | copy-start | bytes 772
  73.6 58.8 %all-to-all-start.4 = ((bf16[2,32,16,768]{3,2,0,1:T(8,128)(2,1)}), bf16[2,32,16,768]{3,2,0,1:T(8,128)(2,1)S(1)}, u32[]{:S(2)}, u32[]{:S(2)}) async-start(bf16[2,32,16,768]{3,2,0,1:T(8,128)(2,1)} %copy.54), calls=%async_computation.4 | async-start | bytes 3145728 | tf_op jit(solution)/shard_map/all_to_all | solution.py:130
  78.3 310.4 %all-gather.16.cloned.1.call-start = ((), (), s32[]{:S(2)}) async-start(), calls=%async_computation.18 | async-start | bytes 5898240 | tf_op jit(solution)/shard_map/all_gather | solution.py:191
  80.7 53.4 %copy-start.8 = (bf16[64,16,768]{2,1,0:T(8,128)(2,1)S(1)}, bf16[64,16,768]{2,1,0:T(8,128)(2,1)}, u32[]{:S(2)}) copy-start(bf16[64,16,768]{2,1,0:T(8,128)(2,1)} %gather_fusion.1) | copy-start | bytes 4718596
  200.3 9.9 copy-start.59
  200.4 10.1 copy-start.60
  200.4 10.3 copy-start.61
  200.4 92.7 %copy-start.44 = (bf16[768]{0:T(1024)(128)(2,1)S(1)}, bf16[768]{0:T(1024)(128)(2,1)}, u32[]{:S(2)}) copy-start(bf16[768]{0:T(1024)(128)(2,1)} %param.39) | copy-start | bytes 4612
  200.4 110.3 %all-to-all-start.1 = ((bf16[64,1,16,768]{3,2,1,0:T(8,128)(2,1)}), bf16[64,1,16,768]{3,2,1,0:T(8,128)(2,1)S(1)}, u32[]{:S(2)}, u32[]{:S(2)}) async-start(bf16[64,1,16,768]{3,2,1,0:T(8,128)(2,1)} %get-tuple-element.278), calls=%async_computation.1 | async-start | bytes 3145728 | tf_op jit(solution)/shard_map/all_to_all | solution.py:141
  204.6 205.0 %all-gather.18.cloned.1.call-start = ((), (), s32[]{:S(2)}) async-start(), calls=%async_computation.19 | async-start | bytes 5898240 | tf_op jit(solution)/shard_map/all_gather | solution.py:193
  205.2 654.1 %reduce-scatter.11.cloned.1.call-start = ((), (), s32[]{:S(2)}) async-start(), calls=%async_computation.22 | async-start | bytes 1474560 | tf_op jit(solution)/shard_map/reduce_scatter | solution.py:326
  292.5 117.2 %copy-start.30 = (f32[768]{0:T(1024)}, f32[768]{0:T(1024)S(1)}, u32[]{:S(2)}) copy-start(f32[768]{0:T(1024)S(1)} %convert_element_type.238) | copy-start | bytes 9220
  387.5 42.6 %copy-start.28 = (f32[576]{0:T(1024)}, f32[576]{0:T(1024)S(1)}, u32[]{:S(2)}) copy-start(f32[576]{0:T(1024)S(1)} %broadcast_multiply_fusion.5) | copy-start | bytes 6916
  388.7 20.9 %copy-start.32 = (f32[576]{0:T(1024)S(1)}, f32[576]{0:T(1024)}, u32[]{:S(2)}) copy-start(f32[576]{0:T(1024)} %add_rsqrt_fusion.1) | copy-start | bytes 6916
  409.6 10.1 copy-start.65
  599.6 259.7 %reduce-scatter.7.cloned.1.call-start = ((), (), s32[]{:S(2)}) async-start(), calls=%async_computation.20 | async-start | bytes 1474560 | tf_op jit(solution)/shard_map/reduce_scatter | solution.py:317
  603.1 256.3 %reduce-scatter.9.cloned.1.call-start = ((), (), s32[]{:S(2)}) async-start(), calls=%async_computation.21 | async-start | bytes 1474560 | tf_op jit(solution)/shard_map/reduce_scatter | solution.py:323
  606.9 252.4 %reduce-scatter.13.cloned.1.call-start = ((), (), s32[]{:S(2)}) async-start(), calls=%async_computation.23 | async-start | bytes 1474560 | tf_op jit(solution)/shard_map/reduce_scatter | solution.py:332
  611.0 278.4 %reduce-scatter.15.cloned.1.call-start = ((), (), s32[]{:S(2)}) async-start(), calls=%async_computation.24 | async-start | bytes 5898240 | tf_op jit(solution)/shard_map/reduce_scatter | solution.py:344
  647.8 60.3 %all-to-all-start.2 = ((bf16[2,32,16,768]{3,2,0,1:T(8,128)(2,1)}), bf16[2,32,16,768]{3,2,0,1:T(8,128)(2,1)S(1)}, u32[]{:S(2)}, u32[]{:S(2)}) async-start(bf16[2,32,16,768]{3,2,0,1:T(8,128)(2,1)} %pad_maximum_fusion), calls=%async_computation.2 | async-start | bytes 3145728 | tf_op jit(solution)/shard_map/all_to_all | solution.py:293
  651.8 347.8 %reduce-scatter.17.cloned.1.call-start = ((), (), s32[]{:S(2)}) async-start(), calls=%async_computation.25 | async-start | bytes 5898240 | tf_op jit(solution)/shard_map/reduce_scatter | solution.py:350
  661.8 50.1 %copy-start.50 = (s32[64]{0:T(128)S(1)}, s32[64]{0:T(128)}, u32[]{:S(2)}) copy-start(s32[64]{0:T(128)} %param.28) | copy-start | bytes 772
  708.0 58.6 %all-to-all-start.6 = ((bf16[2,32,16,768]{3,2,0,1:T(8,128)(2,1)}), bf16[2,32,16,768]{3,2,0,1:T(8,128)(2,1)S(1)}, u32[]{:S(2)}, u32[]{:S(2)}) async-start(bf16[2,32,16,768]{3,2,0,1:T(8,128)(2,1)} %pad_maximum_fusion.1), calls=%async_computation.6 | async-start | bytes 3145728 | tf_op jit(solution)/shard_map/all_to_all | solution.py:300
  715.7 52.7 %copy-start.9 = (bf16[64,16,768]{2,1,0:T(8,128)(2,1)S(1)}, bf16[64,16,768]{2,1,0:T(8,128)(2,1)}, u32[]{:S(2)}) copy-start(bf16[64,16,768]{2,1,0:T(8,128)(2,1)} %gather_fusion.2) | copy-start | bytes 4718596
  854.8 167.5 %all-to-all-start.7 = ((bf16[64,1,16,768]{3,2,1,0:T(8,128)(2,1)}), bf16[64,1,16,768]{3,2,1,0:T(8,128)(2,1)S(1)}, u32[]{:S(2)}, u32[]{:S(2)}) async-start(bf16[64,1,16,768]{3,2,1,0:T(8,128)(2,1)} %get-tuple-element.271), calls=%async_computation.7 | async-start | bytes 3145728 | tf_op jit(solution)/shard_map/all_to_all | solution.py:312
  859.2 219.0 %all-reduce.27.cloned.1.call-start = ((), (), s32[]{:S(2)}) async-start(), calls=%async_computation.26 | async-start | bytes 7077888 | tf_op jit(solution)/shard_map/psum | solution.py:364
  (100 other events, 414.3 us)
Sparse Core Ops, SparseCore 0:
  9.6 59.5 all-gather.9
  70.8 55.0 all-gather.11
  127.5 46.5 all-gather.7
  175.5 35.6 all-gather.13
  212.6 107.3 all-gather.15
  321.4 88.2 all-gather.17
  599.7 27.7 reduce-scatter.10
  629.8 28.1 reduce-scatter.6
  660.4 42.6 reduce-scatter.8
  705.3 50.0 reduce-scatter.12
  757.7 131.7 reduce-scatter.14
  891.6 107.8 reduce-scatter.16
  1003.6 74.5 all-reduce.26
where the time goes:
time: 1100 us; the launch traced here: 1090 us
  waiting for transfers between devices  412 us (37%)
  blocking collectives  269 us (24%)
  matrix products  198 us (18%)
  local copies, waits for them, and re-layouts  78.4 us (7%)
  other arithmetic  44.4 us (4%)
  loops' own time  40.1 us (4%)
  starting transfers between devices  28.9 us (3%)
  between operations  21.8 us (2%)
    reduce_scatter x1, waiting for transfers between devices, on_device(): lax.psum_scatter(grad_wouter.astype(jnp.bfloat16), 'shard', scatter_dimen...  110 us
    unnamed x2, blocking collectives  95.1 us
    all_to_all x1, blocking collectives, on_device(): lax.all_to_all(given_out, ('replica', 'shard'), split_axis=0, concat_axis...  83 us
    dot_general x30, matrix products, dot_left(): lax.dot_general(left_op, right_op, (((0,), (0,)), ((), ())), preferred_el...  79.8 us
    all_to_all x1, blocking collectives, on_device(): lax.all_to_all(chosen_cot, ('replica', 'shard'), split_axis=0, concat_axi...  63.2 us
    dot_general x30, matrix products, dot_rows(): return jnp.dot(left_op, right_op, preferred_element_type=jnp.float32)  60.3 us
    dot_general x42, matrix products, dot_right(): lax.dot_general(left_op, right_op, (((1,), (1,)), ((), ())), preferred_el...  57.7 us
    psum x1, waiting for transfers between devices, on_device(): lax.psum(all_parts[0].astype(jnp.bfloat16), 'replica').astype(jnp.float32)  54.6 us
  transfers between devices with their start and end apart: 19, of which 8 were waited for; matrix products, arithmetic and copies ran while one was open for 14% of the time, Pallas kernels for 0%

commit v1 on v0

v1 whole, which is shorter than its diff:
```python
import functools
import math

import jax
import jax.numpy as jnp
from jax import lax
from jax.experimental import pallas as pl
from jax.experimental.pallas import tpu as pltpu
from jax.sharding import PartitionSpec as P

HEADS = 12
MAXLEN = 512
MINLEN = 64
TILE = 16
NORM_EPS = 1e-12
SCORE_SCALE = 0.125
LOG2E = 1.4426950408889634
EXP_SCALE = SCORE_SCALE * LOG2E
MASK_VALUE = -1e30
BOTH = ("replica", "shard")
BF = jnp.bfloat16
F32 = jnp.float32
I32 = jnp.int32

SMEM = functools.partial(pl.BlockSpec, memory_space=pltpu.SMEM)
VMEM = functools.partial(pl.BlockSpec, memory_space=pltpu.VMEM)
BIG = pltpu.CompilerParams(vmem_limit_bytes=60 * 1024 * 1024)


def dot_rows(left_op, right_op):
    return jnp.dot(left_op, right_op, preferred_element_type=F32)


def dot_left(left_op, right_op):
    return lax.dot_general(left_op, right_op, (((0,), (0,)), ((), ())), preferred_element_type=F32)


def dot_right(left_op, right_op):
    return lax.dot_general(left_op, right_op, (((1,), (1,)), ((), ())), preferred_element_type=F32)


def normalize(values, gain_vec, shift_vec):
    center = values - jnp.mean(values, axis=-1, keepdims=True)
    inverse = lax.rsqrt(jnp.mean(center * center, axis=-1, keepdims=True) + NORM_EPS)
    normed = center * inverse
    return (normed * gain_vec + shift_vec, normed, inverse)


def normalize_back(upstream, normed, inverse, gain_vec):
    scaled = upstream * gain_vec
    centered = (
        scaled
        - jnp.mean(scaled, axis=-1, keepdims=True)
        - normed * jnp.mean(scaled * normed, axis=-1, keepdims=True)
    )
    return (inverse * centered, jnp.sum(upstream * normed, axis=0), jnp.sum(upstream, axis=0))


def gelu_exact(values):
    return 0.5 * values * (1.0 + lax.erf(values * (1.0 / math.sqrt(2.0))))


def gelu_slope(values):
    cumulative = 0.5 * (1.0 + lax.erf(values * (1.0 / math.sqrt(2.0))))
    density = jnp.exp(-0.5 * values * values) * (1.0 / math.sqrt(2.0 * math.pi))
    return cumulative + values * density


def route_kernel(order, lens, me, src_of, dst_of, info, slot_of, keep, len_keep, len_move):
    count = order.shape[0]
    devices = count // 2

    def place(i, carry):
        slot_of[order[i]] = i
        return carry

    def clear(d, carry):
        keep[d] = -1
        return carry

    lax.fori_loop(0, count, place, 0)
    lax.fori_loop(0, devices, clear, 0)

    def start(d, carry):
        def unassigned(seq):
            return keep[lax.shift_right_logical(seq, 1)] < 0

        def step(seq):
            host = lax.shift_right_logical(seq, 1)
            mate = order[lax.bitwise_xor(slot_of[seq], 1)]
            home = lax.shift_right_logical(mate, 1)
            keep[host] = lax.bitwise_and(seq, 1)
            src_of[host] = home
            dst_of[home] = host
            len_keep[host] = lens[seq]
            len_move[host] = lens[mate]
            return lax.bitwise_xor(mate, 1)

        lax.while_loop(unassigned, step, 2 * d)
        return carry

    lax.fori_loop(0, devices, start, 0)
    mine = me[0]
    info[0] = keep[mine]
    info[1] = len_keep[mine]
    info[2] = len_move[mine]
    info[3] = ((len_keep[mine] + (TILE - 1)) // TILE) * TILE


def route(deal_order, seq_lengths, device_pos):
    count = deal_order.shape[0]
    devices = count // 2
    return pl.pallas_call(
        route_kernel,
        out_shape=(
            jax.ShapeDtypeStruct((devices,), I32),
            jax.ShapeDtypeStruct((devices,), I32),
            jax.ShapeDtypeStruct((4,), I32),
        ),
        in_specs=[SMEM(), SMEM(), SMEM()],
        out_specs=(SMEM(), SMEM(), SMEM()),
        scratch_shapes=[
            pltpu.SMEM((count,), I32),
            pltpu.SMEM((devices,), I32),
            pltpu.SMEM((devices,), I32),
            pltpu.SMEM((devices,), I32),
        ],
        name="route",
    )(deal_order, seq_lengths, device_pos.reshape(1))


def pack_kernel(info, kept, moved, out):
    blocks = out.shape[0] // TILE
    seq_blocks = moved.shape[0] // TILE
    shift = info[3] // TILE
    row = lax.broadcasted_iota(I32, (TILE, 1), 0)

    def one(b, carry):
        kb = jnp.minimum(b, seq_blocks - 1)
        mb = jnp.clip(b - shift, 0, seq_blocks - 1)
        here = pl.ds(pl.multiple_of(b * TILE, TILE), TILE)
        a = kept[0, pl.ds(pl.multiple_of(kb * TILE, TILE), TILE), :]
        m = moved[pl.ds(pl.multiple_of(mb * TILE, TILE), TILE), :]
        in_a = b * TILE + row < info[1]
        at = b * TILE - info[3] + row
        in_m = (at >= 0) & (at < info[2])
        out[here, :] = jnp.where(in_a, a, jnp.where(in_m, m, jnp.zeros_like(m)))
        return carry

    lax.fori_loop(0, blocks, one, 0, unroll=False)


def pack(info, given, moved, capacity):
    _, seq_rows, features = given.shape
    return pl.pallas_call(
        pack_kernel,
        out_shape=jax.ShapeDtypeStruct((capacity, features), given.dtype),
        grid_spec=pltpu.PrefetchScalarGridSpec(
            num_scalar_prefetch=1,
            grid=(1,),
            in_specs=[
                pl.BlockSpec((1, seq_rows, features), lambda i, t: (t[0], 0, 0)),
                pl.BlockSpec((seq_rows, features), lambda i, t: (0, 0)),
            ],
            out_specs=pl.BlockSpec((capacity, features), lambda i, t: (0, 0)),
        ),
        name="pack",
    )(info, given, moved)


def unpack_kernel(info, packed, final, moved):
    blocks = packed.shape[0] // TILE
    seq_blocks = moved.shape[0] // TILE
    shift = info[3] // TILE
    row = lax.broadcasted_iota(I32, (TILE, 1), 0)

    def one(b, carry):
        here = pl.ds(pl.multiple_of(b * TILE, TILE), TILE)
        a = packed[here, :]
        mb = jnp.minimum(b + shift, blocks - 1)
        m = packed[pl.ds(pl.multiple_of(mb * TILE, TILE), TILE), :]
        at = b * TILE + row
        final[0, here, :] = jnp.where(at < info[1], a, jnp.zeros_like(a))
        moved[here, :] = jnp.where(at < info[2], m, jnp.zeros_like(m))
        return carry

    lax.fori_loop(0, seq_blocks, one, 0, unroll=False)


def unpack(info, packed, seq_rows):
    capacity, features = packed.shape
    return pl.pallas_call(
        unpack_kernel,
        out_shape=(
            jax.ShapeDtypeStruct((2, seq_rows, features), packed.dtype),
            jax.ShapeDtypeStruct((seq_rows, features), packed.dtype),
        ),
        grid_spec=pltpu.PrefetchScalarGridSpec(
            num_scalar_prefetch=1,
            grid=(1,),
            in_specs=[pl.BlockSpec((capacity, features), lambda i, t: (0, 0))],
            out_specs=(
                pl.BlockSpec((1, seq_rows, features), lambda i, t: (t[0], 0, 0)),
                pl.BlockSpec((seq_rows, features), lambda i, t: (0, 0)),
            ),
        ),
        name="unpack",
    )(info, packed)


def spread_rows(rows, table):
    devices = table.shape[0]
    seq_rows, features = rows.shape
    pieces = rows.reshape(devices, seq_rows // devices, features)
    held = lax.all_to_all(pieces, BOTH, split_axis=0, concat_axis=0, tiled=True)
    held = jnp.take(held, table, axis=0)
    out = lax.all_to_all(held, BOTH, split_axis=0, concat_axis=0, tiled=True)
    return out.reshape(seq_rows, features)


def flip(axis_size, bit):
    return [(i, i ^ bit) for i in range(axis_size)]


def shift_by(axis_size, step):
    return [(i, (i + step) % axis_size) for i in range(axis_size)]


def row_bits(replicas, shard_rows):
    bits = []
    bit = 2
    while bit < replicas and (shard_rows // 2 ** (len(bits) + 1)) % TILE == 0 and len(bits) < 2:
        bits.append(bit)
        bit *= 2
    return tuple(bits)


def row_block(replica, order):
    block = 0
    for bit in order:
        block = 2 * block + lax.bitwise_and(replica // bit, 1)
    return block


def share(held, replicas, order):
    for bit in order:
        held = jnp.concatenate([held, lax.ppermute(held, "replica", flip(replicas, bit))], axis=0)
    return held, lax.ppermute(held, "replica", flip(replicas, 1))


def gather_pieces(piece, replicas, shards, order):
    parts = [piece]
    for step in range(1, shards):
        parts.append(lax.ppermute(piece, "shard", shift_by(shards, step)))
    return share(jnp.stack(parts), replicas, order)


def my_piece(weight, replica, order):
    rows, cols = weight.shape
    take = rows // 2 ** len(order)
    return lax.dynamic_slice(
        weight,
        (row_block(replica, order) * take, lax.bitwise_and(replica, 1) * (cols // 2)),
        (take, cols // 2),
    )


def place_of(block, core_flip, pos, order, shards):
    replica = lax.bitwise_xor(pos[0], core_flip)
    rest = block // shards
    for i, bit in enumerate(order):
        replica = lax.bitwise_xor(replica, lax.bitwise_and(rest // 2**i, 1) * bit)
    shard = lax.rem(pos[1] - lax.rem(block, shards) + shards, shards)
    return replica, shard


def attn_weights_kernel(order, shards, pos, held, recv, w_qkv, w_out, vectors):
    take = (held.shape[1] - TILE) // 4
    half = held.shape[2]
    split = 2 ** len(order)
    groups = half // 128

    for flipped, source in ((0, held), (1, recv)):

        def one(b, carry):
            replica, shard = place_of(b, flipped, pos, order, shards)
            row = pl.multiple_of((shard * split + row_block(replica, order)) * take, TILE)
            core = lax.bitwise_and(replica, 1)
            for w in range(3):
                for g in range(groups):
                    col = pl.multiple_of(core * (half * 3) + g * 384 + w * 128, 128)
                    w_qkv[pl.ds(row, take), pl.ds(col, 128)] = source[
                        b, w * take : (w + 1) * take, g * 128 : (g + 1) * 128
                    ]
            w_out[pl.ds(row, take), pl.ds(pl.multiple_of(core * half, 128), half)] = source[
                b, 3 * take : 4 * take, :
            ]
            return carry

        lax.fori_loop(0, source.shape[0], one, 0)
    for b in range(shards):
        _, shard = place_of(b, 0, pos, order, shards)
        vectors[shard] = held[b, 4 * take :, :]


def attn_weights(pos, held, recv, order, shards, features):
    half = held.shape[2]
    return pl.pallas_call(
        functools.partial(attn_weights_kernel, order, shards),
        out_shape=(
            jax.ShapeDtypeStruct((features, 3 * features), BF),
            jax.ShapeDtypeStruct((features, features), BF),
            jax.ShapeDtypeStruct((shards, TILE, half), BF),
        ),
        in_specs=[SMEM(), VMEM(), VMEM()],
        out_specs=(VMEM(), VMEM(), VMEM()),
        compiler_params=BIG,
        name="attn_weights",
    )(pos, held, recv)


def one_weight_kernel(order, shards, pos, held, recv, out):
    take, half = held.shape[1:]
    split = 2 ** len(order)

    for flipped, source in ((0, held), (1, recv)):

        def one(b, carry):
            replica, shard = place_of(b, flipped, pos, order, shards)
            row = pl.multiple_of((shard * split + row_block(replica, order)) * take, TILE)
            col = pl.multiple_of(lax.bitwise_and(replica, 1) * half, 128)
            out[pl.ds(row, take), pl.ds(col, half)] = source[b]
            return carry

        lax.fori_loop(0, source.shape[0], one, 0)


def one_weight(pos, held, recv, order, shards):
    blocks, take, half = held.shape
    return pl.pallas_call(
        functools.partial(one_weight_kernel, order, shards),
        out_shape=jax.ShapeDtypeStruct((blocks * take, 2 * half), BF),
        in_specs=[SMEM(), VMEM(), VMEM()],
        out_specs=VMEM(),
        compiler_params=BIG,
        name="one_weight",
    )(pos, held, recv)


def row_parts(rows, size):
    return [(at, min(size, rows - at)) for at in range(0, rows, size)]


def split_three(values):
    high = values.astype(BF)
    rest = values - high.astype(F32)
    mid = rest.astype(BF)
    return high, mid, (rest - mid.astype(F32)).astype(BF)


def attend_kernel(info, qkv, out, lse, stats):
    rows = qkv.shape[0]
    lane = lax.broadcasted_iota(I32, (1, 128), 1)
    key_row = lax.broadcasted_iota(I32, (1, rows), 1)
    at = key_row - info[3]
    valid = (key_row < info[1]) | ((at >= 0) & (at < info[2]))
    bias = jnp.where(valid, 0.0, MASK_VALUE).astype(F32)
    keys = qkv[:, 128:256]
    values = qkv[:, 256:384]
    for start, size in row_parts(rows, 128):
        query = qkv[start : start + size, 0:128]
        mixes, totals = [], []
        for h in range(2):
            mine = (lane >= 64) if h else (lane < 64)
            scores = dot_right(jnp.where(mine, query, jnp.zeros_like(query)), keys)
            scores = scores * EXP_SCALE + bias
            top = jnp.max(scores, axis=1, keepdims=True)
            weights = jnp.exp2(scores - top)
            total = jnp.sum(weights, axis=1, keepdims=True)
            mixes.append(dot_rows(weights.astype(BF), values) * (1.0 / total))
            totals.append(top + jnp.log2(total))
        out[start : start + size, :] = jnp.where(lane < 64, mixes[0], mixes[1]).astype(BF)
        stats[start : start + size, :] = jnp.where(lane < 64, totals[0], totals[1])
    pick_row = lax.broadcasted_iota(I32, (TILE, 128), 0)
    pick_lane = lax.broadcasted_iota(I32, (TILE, 128), 1)
    pick = jnp.where(pick_lane == pick_row * 64, 1.0, 0.0).astype(BF)
    across = sum(dot_right(pick, part) for part in split_three(stats[...]))
    lse[...] = across[:8]


def attend(info, qkv):
    rows, width = qkv.shape
    pairs = width // 384
    return pl.pallas_call(
        attend_kernel,
        out_shape=(
            jax.ShapeDtypeStruct((rows, pairs * 128), BF),
            jax.ShapeDtypeStruct((pairs * 8, rows), F32),
        ),
        grid_spec=pltpu.PrefetchScalarGridSpec(
            num_scalar_prefetch=1,
            grid=(pairs,),
            in_specs=[pl.BlockSpec((rows, 384), lambda g, t: (0, g))],
            out_specs=(
                pl.BlockSpec((rows, 128), lambda g, t: (0, g)),
                pl.BlockSpec((8, rows), lambda g, t: (g, 0)),
            ),
            scratch_shapes=[pltpu.VMEM((rows, 128), F32)],
        ),
        cost_estimate=pl.CostEstimate(
            flops=4 * rows * rows * 128 * pairs * 2,
            bytes_accessed=2 * rows * width,
            transcendentals=rows * rows * pairs * 2,
        ),
        name="attend",
    )(info, qkv)


def attend_back_kernel(info, qkv, grad, mix, lse, dqkv, sums, dq):
    rows = qkv.shape[0]
    lane = lax.broadcasted_iota(I32, (1, 128), 1)
    query = qkv[:, 0:128]
    grads = grad[...]
    pick_row = lax.broadcasted_iota(I32, (TILE, 128), 0)
    pick_lane = lax.broadcasted_iota(I32, (TILE, 128), 1)
    pick = jnp.where(lax.shift_right_logical(pick_lane, 6) == pick_row, 1.0, 0.0).astype(BF)
    product = grads.astype(F32) * mix[...].astype(F32)
    row_dots = sum(dot_right(pick, part) for part in split_three(product))
    halves = []
    for h in range(2):
        mine = (lane >= 64) if h else (lane < 64)
        halves.append(
            (
                mine,
                jnp.where(mine, query, jnp.zeros_like(query)),
                jnp.where(mine, grads, jnp.zeros_like(grads)),
                lse[h : h + 1, :],
                row_dots[h : h + 1, :],
            )
        )
    sum_k = jnp.zeros((1, 128), F32)
    sum_v = jnp.zeros((1, 128), F32)
    for index, (start, size) in enumerate(row_parts(rows, 128)):
        keys = qkv[start : start + size, 128:256]
        values = qkv[start : start + size, 256:384]
        row = lax.broadcasted_iota(I32, (size, 1), 0) + start
        at = row - info[3]
        valid = (row < info[1]) | ((at >= 0) & (at < info[2]))
        dk = jnp.zeros((size, 128), F32)
        dv = jnp.zeros((size, 128), F32)
        for h, (mine, query_h, grads_h, lse_h, dots_h) in enumerate(halves):
            keys_h = jnp.where(mine, keys, jnp.zeros_like(keys))
            scores = dot_right(keys, query_h) * EXP_SCALE
            probs = jnp.where(valid, jnp.exp2(scores - lse_h), 0.0)
            dv = dv + dot_rows(probs.astype(BF), grads_h)
            prob_grad = dot_right(values, grads_h)
            score_grad = (probs * (prob_grad - dots_h)).astype(BF)
            dk = dk + dot_rows(score_grad, query_h)
            part = dot_left(score_grad, keys_h)
            if index == 0 and h == 0:
                dq[...] = part
            else:
                dq[...] += part
        dk_low = (dk * SCORE_SCALE).astype(BF)
        dv_low = dv.astype(BF)
        dqkv[start : start + size, 128:256] = dk_low
        dqkv[start : start + size, 256:384] = dv_low
        sum_v = sum_v + jnp.sum(dv_low.astype(F32), axis=0, keepdims=True)
    dq_low = (dq[...] * SCORE_SCALE).astype(BF)
    dqkv[:, 0:128] = dq_low
    sums[...] = jnp.zeros_like(sums)
    sums[0:1, 0:128] = jnp.sum(dq_low.astype(F32), axis=0, keepdims=True)
    sums[0:1, 256:384] = sum_v


def attend_back(info, qkv, grad, mix, lse):
    rows, width = qkv.shape
    pairs = width // 384
    return pl.pallas_call(
        attend_back_kernel,
        out_shape=(
            jax.ShapeDtypeStruct((rows, width), BF),
            jax.ShapeDtypeStruct((pairs * 8, 384), F32),
        ),
        grid_spec=pltpu.PrefetchScalarGridSpec(
            num_scalar_prefetch=1,
            grid=(pairs,),
            in_specs=[
                pl.BlockSpec((rows, 384), lambda g, t: (0, g)),
                pl.BlockSpec((rows, 128), lambda g, t: (0, g)),
                pl.BlockSpec((rows, 128), lambda g, t: (0, g)),
                pl.BlockSpec((8, rows), lambda g, t: (g, 0)),
            ],
            out_specs=(
                pl.BlockSpec((rows, 384), lambda g, t: (0, g)),
                pl.BlockSpec((8, 384), lambda g, t: (g, 0)),
            ),
            scratch_shapes=[pltpu.VMEM((rows, 128), F32)],
        ),
        cost_estimate=pl.CostEstimate(
            flops=10 * rows * rows * 128 * pairs * 2,
            bytes_accessed=6 * rows * width,
            transcendentals=rows * rows * pairs * 2,
        ),
        name="attend_back",
    )(info, qkv, grad, mix, lse)


def core_cols(array, core):
    half = array.shape[1] // 2
    return lax.dynamic_slice_in_dim(array, core * half, half, 1)


def core_sum(left_op, right_op, core, replicas):
    send = dot_left(left_op, core_cols(right_op, 1 - core)).astype(BF)
    got = lax.ppermute(send, "replica", flip(replicas, 1))
    return (dot_left(left_op, core_cols(right_op, core)) + got.astype(F32)).astype(BF)


def reduce_rest(part, replica, shard, replicas, shards, order):
    rows, cols = part.shape
    part = part.reshape(shards, rows // shards, cols)
    for bit in order:
        mine = lax.bitwise_and(replica // bit, 1)
        view = part.reshape(shards, 2, part.shape[1] // 2, cols)
        send = lax.dynamic_index_in_dim(view, 1 - mine, 1, keepdims=False)
        keep = lax.dynamic_index_in_dim(view, mine, 1, keepdims=False)
        got = lax.ppermute(send, "replica", flip(replicas, bit))
        part = (keep.astype(F32) + got.astype(F32)).astype(BF)
    bit = 2
    while bit < replicas:
        if bit not in order:
            got = lax.ppermute(part, "replica", flip(replicas, bit))
            part = (part.astype(F32) + got.astype(F32)).astype(BF)
        bit *= 2
    total = lax.dynamic_index_in_dim(part, shard, 0, keepdims=False).astype(F32)
    for step in range(1, shards):
        send = lax.dynamic_index_in_dim(part, lax.rem(shard + step, shards), 0, keepdims=False)
        total = total + lax.ppermute(send, "shard", shift_by(shards, step)).astype(F32)
    return share(total.astype(BF)[None], replicas, tuple(reversed(order)))


def place_grads_kernel(order, parts, pos, held, recv, *outs):
    take = held.shape[1]
    exchange = tuple(reversed(order))
    for flipped, source in ((0, held), (1, recv)):
        for b in range(source.shape[0]):
            replica, _ = place_of(b, flipped, pos, exchange, 1)
            core = lax.bitwise_and(replica, 1)
            row = pl.multiple_of(row_block(replica, order) * take, TILE)
            for out, pieces in zip(outs, parts):
                half = out.shape[1] // 2
                for to, at, width in pieces:
                    col = pl.multiple_of(core * half + to, 128)
                    out[pl.ds(row, take), pl.ds(col, width)] = source[b, :, at : at + width].astype(F32)


def place_grads(pos, held, recv, order, shapes, parts):
    return pl.pallas_call(
        functools.partial(place_grads_kernel, order, parts),
        out_shape=tuple(jax.ShapeDtypeStruct(shape, F32) for shape in shapes),
        in_specs=[SMEM(), VMEM(), VMEM()],
        out_specs=tuple(VMEM() for _ in shapes),
        compiler_params=BIG,
        name="place_grads",
    )(pos, held, recv)


def sum_all(values, devices):
    bit = 1
    while bit < devices:
        values = values + lax.ppermute(values, BOTH, flip(devices, bit))
        bit *= 2
    return values


def on_device(
    layer_input,
    out_grad,
    seq_lengths,
    deal_order,
    w_query,
    b_query,
    w_key,
    w_value,
    b_value,
    w_output,
    b_output,
    first_gain,
    first_shift,
    w_inner,
    b_inner,
    w_outer,
    b_outer,
    second_gain,
    second_shift,
):
    replicas = lax.axis_size("replica")
    shards = lax.axis_size("shard")
    devices = replicas * shards
    replica = lax.axis_index("replica")
    shard = lax.axis_index("shard")
    core = lax.bitwise_and(replica, 1)
    pos = jnp.stack([replica, shard]).astype(I32)
    seq_rows = layer_input.shape[1]
    features = layer_input.shape[2]
    hidden = w_inner.shape[1]
    capacity = MAXLEN + MINLEN + TILE
    src_of, dst_of, info = route(deal_order, seq_lengths, replica * shards + shard)
    other = 1 - info[0]

    moved_in = spread_rows(lax.dynamic_index_in_dim(layer_input, other, 0, keepdims=False), src_of)
    packed_in = pack(info, layer_input, moved_in, capacity)
    cot_rows = lax.dynamic_index_in_dim(out_grad, other, 0, keepdims=False)
    cot_rows, _ = lax.optimization_barrier((cot_rows, moved_in))
    packed_cot = pack(info, out_grad, spread_rows(cot_rows, src_of), capacity)

    bits = row_bits(replicas, w_query.shape[0])
    order_a, order_b = bits, tuple(reversed(bits))
    shard_vec = jnp.concatenate(
        [
            b_query,
            b_value,
            b_output,
            first_gain,
            first_shift,
            b_outer,
            second_gain,
            second_shift,
            b_inner,
        ]
    )
    half = features // 2
    vec_rows = shard_vec.reshape(-1, half) if shard_vec.shape[0] % half == 0 else None
    if vec_rows is None:
        lacking = -shard_vec.shape[0] % half
        vec_rows = jnp.pad(shard_vec, (0, lacking)).reshape(-1, half)
    vec_rows = jnp.pad(vec_rows, ((0, TILE - vec_rows.shape[0]), (0, 0)))
    attn_piece = jnp.concatenate(
        [my_piece(w, replica, order_a) for w in (w_query, w_key, w_value, w_output)] + [vec_rows],
        axis=0,
    )
    held, recv = gather_pieces(attn_piece, replicas, shards, order_a)
    wqkv_full, wo_full, vectors = attn_weights(pos, held, recv, order_a, shards, features)
    inner_piece = my_piece(w_inner, replica, order_b)
    wi_full = one_weight(pos, *gather_pieces(inner_piece, replicas, shards, order_b), order_b, shards)
    outer_piece = my_piece(w_outer, replica, order_a)
    wout_full = one_weight(pos, *gather_pieces(outer_piece, replicas, shards, order_a), order_a, shards)
    flat = vectors.reshape(shards, -1)
    per = features // shards
    named = [flat[:, i * per : (i + 1) * per].reshape(features).astype(F32) for i in range(8)]
    bq, bv, bo, gain_one, shift_one, bout, gain_two, shift_two = named
    bi = flat[:, 8 * per : 8 * per + hidden // shards].reshape(hidden).astype(F32)
    pairs = features // 128
    bqkv = jnp.stack(
        [bq.reshape(pairs, 128), jnp.zeros((pairs, 128), F32), bv.reshape(pairs, 128)], axis=1
    ).reshape(3 * features)

    qkv = (dot_rows(packed_in, wqkv_full) + bqkv).astype(BF)
    mix_low, lse = attend(info, qkv)
    branch = dot_rows(mix_low, wo_full) + bo
    first_out, normed_one, inverse_one = normalize(
        packed_in.astype(F32) + branch, gain_one, shift_one
    )
    hidden_low = first_out.astype(BF)
    inner_pre = dot_rows(hidden_low, wi_full) + bi
    act_low = gelu_exact(inner_pre).astype(BF)
    outer_out = dot_rows(act_low, wout_full) + bout
    packed_out, normed_two, inverse_two = normalize(first_out + outer_out, gain_two, shift_two)
    final_out, out_moved = unpack(info, packed_out.astype(BF), seq_rows)
    out_back = spread_rows(out_moved, dst_of)
    final_out = lax.dynamic_update_slice(final_out, out_back[None], (other, 0, 0))

    second_back, grad_secondgain, grad_secondshift = normalize_back(
        packed_cot.astype(F32), normed_two, inverse_two, gain_two
    )
    outer_grad = second_back.astype(BF)
    grad_bouter = jnp.sum(outer_grad.astype(F32), axis=0)
    inner_grad = (dot_right(outer_grad, wout_full) * gelu_slope(inner_pre)).astype(BF)
    grad_binner = jnp.sum(inner_grad.astype(F32), axis=0)
    part_outer = core_sum(act_low, outer_grad, core, replicas)
    part_inner = core_sum(hidden_low, inner_grad, core, replicas)
    first_total = second_back + dot_right(inner_grad, wi_full)
    first_back, grad_firstgain, grad_firstshift = normalize_back(
        first_total, normed_one, inverse_one, gain_one
    )
    branch_grad = first_back.astype(BF)
    grad_boutput = jnp.sum(branch_grad.astype(F32), axis=0)
    part_output = core_sum(mix_low, branch_grad, core, replicas)
    mix_grad = dot_right(branch_grad, wo_full).astype(BF)
    dqkv, dqkv_sums = attend_back(info, qkv, mix_grad, mix_low, lse)
    input_packed = first_back + dot_right(dqkv, wqkv_full)
    final_back, back_moved = unpack(info, input_packed.astype(BF), seq_rows)
    back_rows = spread_rows(back_moved, dst_of)
    final_back = lax.dynamic_update_slice(final_back, back_rows[None], (other, 0, 0))
    part_qkv = core_sum(packed_in, dqkv, core, replicas)

    inner_half = hidden // 2
    shard_rows = features // shards
    (grad_wouter,) = place_grads(
        pos,
        *reduce_rest(part_outer, replica, shard, replicas, shards, order_a),
        order_a,
        [(hidden // shards, features)],
        [[(0, 0, half)]],
    )
    grad_winner, grad_woutput = place_grads(
        pos,
        *reduce_rest(
            jnp.concatenate([part_inner, part_output], axis=1),
            replica,
            shard,
            replicas,
            shards,
            order_b,
        ),
        order_b,
        [(shard_rows, hidden), (shard_rows, features)],
        [[(0, 0, inner_half)], [(0, inner_half, half)]],
    )
    grad_wquery, grad_wkey, grad_wvalue = place_grads(
        pos,
        *reduce_rest(part_qkv, replica, shard, replicas, shards, order_a),
        order_a,
        [(shard_rows, features)] * 3,
        [[(g * 128, g * 384 + w * 128, 128) for g in range(half // 128)] for w in range(3)],
    )
    sums = dqkv_sums.reshape(pairs, 8, 3, 128)[:, 0]
    grad_bquery = sums[:, 0].reshape(features)
    grad_bvalue = sums[:, 2].reshape(features)
    totals = sum_all(
        jnp.concatenate(
            [
                v.reshape(-1, 128)
                for v in (
                    grad_bquery,
                    grad_bvalue,
                    grad_boutput,
                    grad_firstgain,
                    grad_firstshift,
                    grad_bouter,
                    grad_secondgain,
                    grad_secondshift,
                    grad_binner,
                )
            ],
            axis=0,
        ),
        devices,
    ).reshape(-1)
    vec = [
        lax.dynamic_slice_in_dim(totals, i * features + shard * per, per, 0) for i in range(8)
    ]
    grad_binner = lax.dynamic_slice_in_dim(
        totals, 8 * features + shard * (hidden // shards), hidden // shards, 0
    )
    return (
        final_out,
        final_back,
        grad_wquery,
        vec[0],
        grad_wkey,
        grad_wvalue,
        vec[1],
        grad_woutput,
        vec[2],
        vec[3],
        vec[4],
        grad_winner,
        grad_binner,
        grad_wouter,
        vec[5],
        vec[6],
        vec[7],
    )


def solution(mesh):
    rows = P(BOTH, None, None)
    matrix = P("shard", None)
    vector = P("shard")
    in_specs = (
        rows,
        rows,
        P(),
        P(),
        matrix,
        vector,
        matrix,
        matrix,
        vector,
        matrix,
        vector,
        vector,
        vector,
        matrix,
        vector,
        matrix,
        vector,
        vector,
        vector,
    )
    out_specs = (
        rows,
        rows,
        matrix,
        vector,
        matrix,
        matrix,
        vector,
        matrix,
        vector,
        vector,
        vector,
        matrix,
        vector,
        matrix,
        vector,
        vector,
        vector,
    )
    return jax.shard_map(
        on_device, mesh=mesh, in_specs=in_specs, out_specs=out_specs, check_vma=False
    )
```

time: 1100 us -> 516 us (0.47)
  blocking collectives: 269 us -> 0 us
  waiting for transfers between devices: 412 us -> 143 us
  matrix products: 198 us -> 64.5 us
  Pallas kernels: 0 us -> 94.1 us
  starting transfers between devices: 28.9 us -> 118 us
  loops' own time: 40.1 us -> 0 us
  other arithmetic: 44.4 us -> 24.7 us
  between operations: 21.8 us -> 3.11 us
  local copies, waits for them, and re-layouts: 78.4 us -> 61.3 us
    all_to_all x6 -> x8, waiting for transfers between devices: 201 us -> 20.6 us  [the longest x4 20.5 us: spread_rows(): held = lax.all_to_all(pieces, BOTH, split_axis=0, concat_axis=0, tiled=True)]
    all_to_all x2 -> x0, blocking collectives: 146 us -> none  [the longest x1 83 us: on_device(): lax.all_to_all(given_out, ('replica', 'shard'), split_axis=0, concat_axis...]
    reduce_scatter x6 -> x0, waiting for transfers between devices: 140 us -> none  [the longest x1 110 us: on_device(): lax.psum_scatter(grad_wouter.astype(jnp.bfloat16), 'shard', scatter_dimen...]
    ppermute x0 -> x51, waiting for transfers between devices: none -> 122 us  [the longest x12 66.1 us: share(): lax.ppermute(held, 'replica', flip(replicas, bit))]
    unnamed x2 -> x0, blocking collectives: 95.1 us -> none
    pallas_call x0 -> x13, Pallas kernels: none -> 94.1 us  [the longest x1 28.3 us: attend_back(): pl.pallas_call(attend_back_kernel, out_shape=(jax.ShapeDtypeStruct((rows,...]
    ppermute x0 -> x51, starting transfers between devices: none -> 88.8 us  [the longest x9 38.5 us: gather_pieces(): parts.append(lax.ppermute(piece, 'shard', shift_by(shards, step)))]
    psum x1 -> x0, waiting for transfers between devices: 54.6 us -> none  [on_device(): lax.psum(all_parts[0].astype(jnp.bfloat16), 'replica').astype(jnp.float32)]
  transfers between devices with their start and end apart: 19 -> 59, of which waited for: 8 -> 18; matrix products, arithmetic and copies ran while one was open for 14% -> 22% of each run, Pallas kernels for 0% -> 12%
where the time goes in v1:
time: 516 us; the launch traced here: 509 us
  waiting for transfers between devices  143 us (28%)
  starting transfers between devices  118 us (23%)
  Pallas kernels  94.1 us (18%)
  matrix products  64.5 us (12%)
  local copies, waits for them, and re-layouts  61.3 us (12%)
  other arithmetic  24.7 us (5%)
    ppermute x12, waiting for transfers between devices, share(): lax.ppermute(held, 'replica', flip(replicas, bit))  66.1 us
    ppermute x9, starting transfers between devices, gather_pieces(): parts.append(lax.ppermute(piece, 'shard', shift_by(shards, step)))  38.5 us
    pallas_call x1, Pallas kernels, attend_back(): pl.pallas_call(attend_back_kernel, out_shape=(jax.ShapeDtypeStruct((rows,...  28.3 us
    dot_general x8, matrix products, dot_left(): lax.dot_general(left_op, right_op, (((0,), (0,)), ((), ())), preferred_el...  28 us
    unnamed x102, local copies, waits for them, and re-layouts  24.3 us
    ppermute x9, waiting for transfers between devices, reduce_rest(): lax.ppermute(send, 'shard', shift_by(shards, step)).astype(F32)  24.2 us
    ppermute x6, waiting for transfers between devices, reduce_rest(): got = lax.ppermute(send, 'replica', flip(replicas, bit))  24.1 us
    pallas_call x1, Pallas kernels, attend(): pl.pallas_call(attend_kernel, out_shape=(jax.ShapeDtypeStruct((rows, pair...  22.7 us
  transfers between devices with their start and end apart: 59, of which 18 were waited for; matrix products, arithmetic and copies ran while one was open for 22% of the time, Pallas kernels for 12%

profile of v1, /device:TPU:0, one launch (start us, length us, event | category | flops | bytes accessed | tf_op | source)
XLA Modules:
  0.0 509.0 jit_solution(1581089417371317609)
XLA Ops:
  0.7 6.1 %concatenate.57 = bf16[2304]{0:T(1024)(128)(2,1)S(1)} concatenate(bf16[192]{0:T(256)(128)(2,1)} %param.26, bf16[192]{0:T(256)(128)(2,1)} %param.29, bf16[192]{0:T(256)(128)(2,1)} %param.31, bf16[192]{0:T(256)(128)(2,1)} %param.32, bf16[192]{0:T(256)(128)(2,1)} %param.33, bf16[192]{0:T(256)(128)(2,1)} %param.37, bf16[192]{0:T(256)(128)(2,1)} %param.38, bf16[192]{0:T(256)(128)(2,1)} %param.39, ...), dimensions={0} | concatenate | bytes 9216 | tf_op jit(solution)/shard_map/concatenate | solution.py:620
  9.9 5.1 %collective-permute-start.2 = (bf16[208,384]{1,0:T(8,128)(2,1)S(1)}, bf16[208,384]{1,0:T(8,128)(2,1)}, u32[]{:S(2)}, u32[]{:S(2)}) collective-permute-start(bf16[208,384]{1,0:T(8,128)(2,1)S(1)} %constant_dynamic-update-slice_fusion), channel_id=1, source_target_pairs={{0,3},{1,0},{2,1},{3,2},{4,7},{5,4},{6,5},{7,6},{8,11},{9,8},{10,9... | collective-permute-start | bytes 479240 | tf_op jit(solution)/shard_map/ppermute | solution.py:254
  28.0 4.0 all-to-all-start
  38.7 4.1 collective-permute-done.7
  42.8 11.4 %collective-permute-start.12 = (bf16[192,384]{1,0:T(8,128)(2,1)S(1)}, bf16[192,384]{1,0:T(8,128)(2,1)S(1)}, u32[]{:S(2)}, u32[]{:S(2)}) collective-permute-start(bf16[192,384]{1,0:T(8,128)(2,1)S(1)} %get-tuple-element.72), channel_id=1, source_target_pairs={{0,1},{1,2},{2,3},{3,0},{4,5},{5,6},{6,7},{7,4},{8,9},{9,10},{10,1... | collective-permute-start | bytes 442376 | tf_op jit(solution)/shard_map/ppermute | solution.py:254
  55.3 13.4 %collective-permute-start = (bf16[208,384]{1,0:T(8,128)(2,1)S(1)}, bf16[208,384]{1,0:T(8,128)(2,1)S(1)}, u32[]{:S(2)}, u32[]{:S(2)}) collective-permute-start(bf16[208,384]{1,0:T(8,128)(2,1)S(1)} %constant_dynamic-update-slice_fusion), channel_id=1, source_target_pairs={{0,1},{1,2},{2,3},{3,0},{4,5},{5,6},{6,7},{7,4},{8,9},{9,10},{10,1... | collective-permute-start | bytes 479240 | tf_op jit(solution)/shard_map/ppermute | solution.py:254
  90.7 11.6 %collective-permute-done.3 = bf16[4,208,384]{2,1,0:T(8,128)(2,1)S(1)} collective-permute-done((bf16[4,208,384]{2,1,0:T(8,128)(2,1)S(1)}, bf16[4,208,384]{2,1,0:T(8,128)(2,1)S(1)}, u32[]{:S(2)}, u32[]{:S(2)}) %collective-permute-start.3) | collective-permute-done | bytes 639008 | tf_op jit(solution)/shard_map/ppermute | solution.py:247
  108.6 24.9 %collective-permute-done.10 = bf16[8,48,1536]{2,1,0:T(8,128)(2,1)} collective-permute-done((bf16[8,48,1536]{2,1,0:T(8,128)(2,1)}, bf16[8,48,1536]{2,1,0:T(8,128)(2,1)}, u32[]{:S(2)}, u32[]{:S(2)}) %collective-permute-start.10) | collective-permute-done | bytes 1179680 | tf_op jit(solution)/shard_map/ppermute | solution.py:247
  138.7 13.5 %collective-permute-done.4 = bf16[8,208,384]{2,1,0:T(8,128)(2,1)} collective-permute-done((bf16[8,208,384]{2,1,0:T(8,128)(2,1)}, bf16[8,208,384]{2,1,0:T(8,128)(2,1)}, u32[]{:S(2)}, u32[]{:S(2)}) %collective-permute-start.4) | collective-permute-done | bytes 1277984 | tf_op jit(solution)/shard_map/ppermute | solution.py:247
  163.0 5.8 %one_weight.2 = bf16[768,3072]{1,0:T(8,128)(2,1)} custom-call(s32[2]{0:T(128)} %pad_add_fusion.pos, bf16[16,48,1536]{2,1,0:T(8,128)(2,1)} %constant_dynamic-update-slice_fusion.21.held, bf16[16,48,1536]{2,1,0:T(8,128)(2,1)} %collective-permute-done.11.recv), custom_call_target="tpu_custom_call" | custom-call | tf_op jit(solution)/shard_map/one_weight/pallas_call | solution.py:340
  168.8 5.9 %one_weight.3 = bf16[3072,768]{1,0:T(8,128)(2,1)} custom-call(s32[2]{0:T(128)} %pad_add_fusion.pos, bf16[16,192,384]{2,1,0:T(8,128)(2,1)} %constant_dynamic-update-slice_fusion.32.held, bf16[16,192,384]{2,1,0:T(8,128)(2,1)} %collective-permute-done.17.recv), custom_call_target="tpu_custom_call" | custom-call | tf_op jit(solution)/shard_map/one_weight/pallas_call | solution.py:340
  179.4 4.7 all-to-all-start.5
  184.1 6.4 %attn_weights.1 = (bf16[768,2304]{1,0:T(8,128)(2,1)}, bf16[768,768]{1,0:T(8,128)(2,1)}, bf16[4,16,384]{2,1,0:T(8,128)(2,1)}) custom-call(s32[2]{0:T(128)} %pad_add_fusion.pos, bf16[16,208,384]{2,1,0:T(8,128)(2,1)} %constant_dynamic-update-slice_fusion.10.held, bf16[16,208,384]{2,1,0:T(8,128)(2,1)} %collective-permute-done.5.recv), custom_call_target="tpu_custom_call" | custom-call | tf_op jit(solution)/shard_map/attn_weights/pallas_call | solution.py:308
  192.2 5.9 %add_convert_fusion.qkv = bf16[592,2304]{1,0:T(8,128)(2,1)} fusion(bf16[592,768]{1,0:T(8,128)(2,1)S(1)} %copy-done.16, bf16[768,2304]{1,0:T(8,128)(2,1)} %get-tuple-element.40, f32[2304]{0:T(1024)S(1)} %add.355), kind=kOutput, calls=%fused_computation.14 | convolution fusion | flops 2097782784 | bytes 7185408 | tf_op jit(solution)/shard_map/dot_general | solution.py:31
  198.1 22.7 %attend.1 = (bf16[592,768]{1,0:T(8,128)(2,1)}, f32[48,592]{1,0:T(8,128)}) custom-call(s32[4]{0:T(128)} %get-tuple-element.38.info, bf16[592,2304]{1,0:T(8,128)(2,1)} %add_convert_fusion.qkv), custom_call_target="tpu_custom_call" | custom-call | flops 2153250816 | bytes 2727936 | tf_op jit(solution)/shard_map/attend/pallas_call | solution.py:394
  224.1 7.4 %multiply_convert_fusion = (bf16[592,3072]{1,0:T(8,128)(2,1)S(1)}, f32[592,3072]{1,0:T(8,128)}) fusion(f32[3072]{0:T(1024)S(1)} %reshape.274, bf16[592,768]{1,0:T(8,128)(2,1)S(1)} %fusion.21, bf16[768,3072]{1,0:T(8,128)(2,1)} %one_weight.2), kind=kOutput, calls=%fused_computation.12 | convolution fusion | flops 2804318208 | bytes 16551936 | tf_op jit(solution)/shard_map/dot_general | solution.py:31
  245.3 8.5 %convert_reduce_fusion = (f32[3072]{0:T(1024)S(1)}, bf16[592,3072]{1,0:T(8,128)(2,1)S(1)}) fusion(f32[592,3072]{1,0:T(8,128)} %get-tuple-element.134, f32[3072]{0:T(1024)S(1)} %reshape.274, bf16[592,768]{1,0:T(8,128)(2,1)S(1)} %get-tuple-element.67, bf16[3072,768]{1,0:T(8,128)(2,1)} %one_weight.3), kind=kOutput, calls=%fused_computation.11 | convolution fusion | flops 2817045504 | bytes 16564224 | tf_op jit(solution)/shard_map/dot_general | solution.py:39
  261.5 28.3 %attend_back.1 = (bf16[592,2304]{1,0:T(8,128)(2,1)}, f32[48,384]{1,0:T(8,128)}) custom-call(s32[4]{0:T(128)} %get-tuple-element.38.info, bf16[592,2304]{1,0:T(8,128)(2,1)} %add_convert_fusion.qkv, bf16[592,768]{1,0:T(8,128)(2,1)} %convolution_convert_fusion.3.grad, bf16[592,768]{1,0:T(8,128)(2,1)} %get-tuple-element.42.mix, f32[48,592]{1,0:T(8,128)} %get-tuple-element.48.lse), custom_call_target="tpu_custom_call" | custom-call | flops 5383127040 | bytes 8183808 | tf_op jit(solution)/shard_map/attend_back/pallas_call | solution.py:479
  290.7 4.4 convolution_convert_fusion.2
  301.7 5.3 %convolution_convert_fusion.1 = bf16[768,1536]{1,0:T(8,128)(2,1)} fusion(bf16[592,768]{1,0:T(8,128)(2,1)} %copy-done.18, bf16[592,3072]{1,0:T(8,128)(2,1)} %copy-done.32, s32[]{:T(128)S(6)} %select_n.172), kind=kOutput, calls=%fused_computation.19 | convolution fusion | flops 1397882880 | bytes 5087236 | tf_op jit(solution)/shard_map/dot_general | solution.py:35
  319.0 4.2 all-to-all-start.6
  343.5 5.0 all-to-all-start.2
  348.5 4.2 add_convert_fusion.2
  353.0 11.8 %collective-permute-done.19 = bf16[4,96,1152]{2,1,0:T(8,128)(2,1)} collective-permute-done((bf16[4,96,1152]{2,1,0:T(8,128)(2,1)}, bf16[4,96,1152]{2,1,0:T(8,128)(2,1)}, u32[]{:S(2)}, u32[]{:S(2)}) %collective-permute-start.19) | collective-permute-done | bytes 884768 | tf_op jit(solution)/shard_map/ppermute | solution.py:528
  376.1 17.5 %all-to-all-done.2 = bf16[32,16,768]{2,1,0:T(8,128)(2,1)} async-done(((bf16[32,16,768]{2,1,0:T(8,128)(2,1)}), bf16[32,16,768]{2,1,0:T(8,128)(2,1)}, u32[]{:S(2)}, u32[]{:S(2)}) %all-to-all-start.2) | async-done | bytes 786464 | tf_op jit(solution)/shard_map/all_to_all | solution.py:215
  410.3 10.0 %collective-permute-done.34 = bf16[4,96,1920]{2,1,0:T(8,128)(2,1)} collective-permute-done((bf16[4,96,1920]{2,1,0:T(8,128)(2,1)}, bf16[4,96,1920]{2,1,0:T(8,128)(2,1)}, u32[]{:S(2)}, u32[]{:S(2)}) %collective-permute-start.34) | collective-permute-done | bytes 1474592 | tf_op jit(solution)/shard_map/ppermute | solution.py:528
  424.1 8.3 %collective-permute-done.22 = bf16[48,1152]{1,0:T(8,128)(2,1)S(1)} collective-permute-done((bf16[48,1152]{1,0:T(8,128)(2,1)S(1)}, bf16[48,1152]{1,0:T(8,128)(2,1)S(1)}, u32[]{:S(2)}, u32[]{:S(2)}) %collective-permute-start.22) | collective-permute-done | bytes 110624 | tf_op jit(solution)/shard_map/ppermute | solution.py:539
  440.3 8.4 %collective-permute-start.46 = (bf16[192,384]{1,0:T(8,128)(2,1)S(1)}, bf16[192,384]{1,0:T(8,128)(2,1)S(1)}, u32[]{:S(2)}, u32[]{:S(2)}) collective-permute-start(bf16[192,384]{1,0:T(8,128)(2,1)S(1)} %get-tuple-element.83), channel_id=1, source_target_pairs={{0,2},{1,3},{2,0},{3,1},{4,6},{5,7},{6,4},{7,5},{8,10},{9,11},{10,... | collective-permute-start | bytes 442376 | tf_op jit(solution)/shard_map/ppermute | solution.py:539
  453.0 7.0 %collective-permute-done.46 = bf16[192,384]{1,0:T(8,128)(2,1)S(1)} collective-permute-done((bf16[192,384]{1,0:T(8,128)(2,1)S(1)}, bf16[192,384]{1,0:T(8,128)(2,1)S(1)}, u32[]{:S(2)}, u32[]{:S(2)}) %collective-permute-start.46) | collective-permute-done | bytes 147488 | tf_op jit(solution)/shard_map/ppermute | solution.py:539
  461.5 9.0 %collective-permute-done.37 = bf16[48,1920]{1,0:T(8,128)(2,1)S(1)} collective-permute-done((bf16[48,1920]{1,0:T(8,128)(2,1)S(1)}, bf16[48,1920]{1,0:T(8,128)(2,1)S(1)}, u32[]{:S(2)}, u32[]{:S(2)}) %collective-permute-start.37) | collective-permute-done | bytes 184352 | tf_op jit(solution)/shard_map/ppermute | solution.py:539
  479.6 5.7 %collective-permute-done.25 = bf16[2,48,1152]{2,1,0:T(8,128)(2,1)S(1)} collective-permute-done((bf16[2,48,1152]{2,1,0:T(8,128)(2,1)S(1)}, bf16[2,48,1152]{2,1,0:T(8,128)(2,1)S(1)}, u32[]{:S(2)}, u32[]{:S(2)}) %collective-permute-start.25) | collective-permute-done | bytes 221216 | tf_op jit(solution)/shard_map/ppermute | solution.py:247
  485.4 8.8 %collective-permute-done.49 = bf16[2,192,384]{2,1,0:T(8,128)(2,1)S(1)} collective-permute-done((bf16[2,192,384]{2,1,0:T(8,128)(2,1)S(1)}, bf16[2,192,384]{2,1,0:T(8,128)(2,1)S(1)}, u32[]{:S(2)}, u32[]{:S(2)}) %collective-permute-start.49) | collective-permute-done | bytes 294944 | tf_op jit(solution)/shard_map/ppermute | solution.py:247
  (312 shorter events, 206.3 us)
Async XLA Ops:
  9.9 71.0 %collective-permute-start.2 = (bf16[208,384]{1,0:T(8,128)(2,1)S(1)}, bf16[208,384]{1,0:T(8,128)(2,1)}, u32[]{:S(2)}, u32[]{:S(2)}) collective-permute-start(bf16[208,384]{1,0:T(8,128)(2,1)S(1)} %constant_dynamic-update-slice_fusion), channel_id=1, source_target_pairs={{0,3},{1,0},{2,1},{3,2},{4,7},{5,4},{6,5},{7,6},{8,11},{9,8},{10,9... | collective-permute-start | bytes 479240 | tf_op jit(solution)/shard_map/ppermute | solution.py:254
  15.1 65.9 %collective-permute-start.1 = (bf16[208,384]{1,0:T(8,128)(2,1)S(1)}, bf16[208,384]{1,0:T(8,128)(2,1)}, u32[]{:S(2)}, u32[]{:S(2)}) collective-permute-start(bf16[208,384]{1,0:T(8,128)(2,1)S(1)} %constant_dynamic-update-slice_fusion), channel_id=1, source_target_pairs={{0,2},{1,3},{2,0},{3,1},{4,6},{5,7},{6,4},{7,5},{8,10},{9,11},{10,... | collective-permute-start | bytes 479240 | tf_op jit(solution)/shard_map/ppermute | solution.py:254
  17.1 25.7 %collective-permute-start.7 = (bf16[48,1536]{1,0:T(8,128)(2,1)S(1)}, bf16[48,1536]{1,0:T(8,128)(2,1)}, u32[]{:S(2)}, u32[]{:S(2)}) collective-permute-start(bf16[48,1536]{1,0:T(8,128)(2,1)S(1)} %get-tuple-element.74), channel_id=1, source_target_pairs={{0,2},{1,3},{2,0},{3,1},{4,6},{5,7},{6,4},{7,5},{8,10},{9,11},{10,... | collective-permute-start | bytes 442376 | tf_op jit(solution)/shard_map/ppermute | solution.py:254
  19.6 23.2 %collective-permute-start.6 = (bf16[48,1536]{1,0:T(8,128)(2,1)S(1)}, bf16[48,1536]{1,0:T(8,128)(2,1)}, u32[]{:S(2)}, u32[]{:S(2)}) collective-permute-start(bf16[48,1536]{1,0:T(8,128)(2,1)S(1)} %get-tuple-element.74), channel_id=1, source_target_pairs={{0,1},{1,2},{2,3},{3,0},{4,5},{5,6},{6,7},{7,4},{8,9},{9,10},{10,1... | collective-permute-start | bytes 442376 | tf_op jit(solution)/shard_map/ppermute | solution.py:254
  28.0 76.1 %all-to-all-start = ((bf16[32,16,768]{2,1,0:T(8,128)(2,1)}), bf16[32,16,768]{2,1,0:T(8,128)(2,1)S(1)}, u32[]{:S(2)}, u32[]{:S(2)}) async-start(bf16[32,16,768]{2,1,0:T(8,128)(2,1)} %bitcast.3), calls=%async_computation | async-start | bytes 1572864 | tf_op jit(solution)/shard_map/all_to_all | solution.py:215
  42.8 28.0 %collective-permute-start.13 = (bf16[192,384]{1,0:T(8,128)(2,1)S(1)}, bf16[192,384]{1,0:T(8,128)(2,1)S(1)}, u32[]{:S(2)}, u32[]{:S(2)}) collective-permute-start(bf16[192,384]{1,0:T(8,128)(2,1)S(1)} %get-tuple-element.72), channel_id=1, source_target_pairs={{0,2},{1,3},{2,0},{3,1},{4,6},{5,7},{6,4},{7,5},{8,10},{9,11},{10,... | collective-permute-start | bytes 442376 | tf_op jit(solution)/shard_map/ppermute | solution.py:254
  42.8 29.5 %collective-permute-start.12 = (bf16[192,384]{1,0:T(8,128)(2,1)S(1)}, bf16[192,384]{1,0:T(8,128)(2,1)S(1)}, u32[]{:S(2)}, u32[]{:S(2)}) collective-permute-start(bf16[192,384]{1,0:T(8,128)(2,1)S(1)} %get-tuple-element.72), channel_id=1, source_target_pairs={{0,1},{1,2},{2,3},{3,0},{4,5},{5,6},{6,7},{7,4},{8,9},{9,10},{10,1... | collective-permute-start | bytes 442376 | tf_op jit(solution)/shard_map/ppermute | solution.py:254
  55.3 25.6 %collective-permute-start = (bf16[208,384]{1,0:T(8,128)(2,1)S(1)}, bf16[208,384]{1,0:T(8,128)(2,1)S(1)}, u32[]{:S(2)}, u32[]{:S(2)}) collective-permute-start(bf16[208,384]{1,0:T(8,128)(2,1)S(1)} %constant_dynamic-update-slice_fusion), channel_id=1, source_target_pairs={{0,1},{1,2},{2,3},{3,0},{4,5},{5,6},{6,7},{7,4},{8,9},{9,10},{10,1... | collective-permute-start | bytes 479240 | tf_op jit(solution)/shard_map/ppermute | solution.py:254
  87.6 45.8 %collective-permute-start.10 = (bf16[8,48,1536]{2,1,0:T(8,128)(2,1)}, bf16[8,48,1536]{2,1,0:T(8,128)(2,1)}, u32[]{:S(2)}, u32[]{:S(2)}) collective-permute-start(bf16[8,48,1536]{2,1,0:T(8,128)(2,1)} %get-tuple-element.86), channel_id=1, source_target_pairs={{0,8},{4,12},{8,0},{12,4},{16,24},{20,28},{24,16},{28,20},{1,9},{5... | collective-permute-start | bytes 3538952 | tf_op jit(solution)/shard_map/ppermute | solution.py:247
  90.2 45.6 %collective-permute-start.16 = (bf16[8,192,384]{2,1,0:T(8,128)(2,1)}, bf16[8,192,384]{2,1,0:T(8,128)(2,1)}, u32[]{:S(2)}, u32[]{:S(2)}) collective-permute-start(bf16[8,192,384]{2,1,0:T(8,128)(2,1)} %get-tuple-element.84), channel_id=1, source_target_pairs={{0,16},{4,20},{8,24},{12,28},{16,0},{20,4},{24,8},{28,12},{1,17},{... | collective-permute-start | bytes 3538952 | tf_op jit(solution)/shard_map/ppermute | solution.py:247
  103.5 48.7 %collective-permute-start.4 = (bf16[8,208,384]{2,1,0:T(8,128)(2,1)}, bf16[8,208,384]{2,1,0:T(8,128)(2,1)}, u32[]{:S(2)}, u32[]{:S(2)}) collective-permute-start(bf16[8,208,384]{2,1,0:T(8,128)(2,1)} %get-tuple-element.79), channel_id=1, source_target_pairs={{0,16},{4,20},{8,24},{12,28},{16,0},{20,4},{24,8},{28,12},{1,17},{... | collective-permute-start | bytes 3833864 | tf_op jit(solution)/shard_map/ppermute | solution.py:247
  105.7 49.9 %all-to-all-start.1 = ((bf16[32,16,768]{2,1,0:T(8,128)(2,1)}), bf16[32,16,768]{2,1,0:T(8,128)(2,1)S(1)}, u32[]{:S(2)}, u32[]{:S(2)}) async-start(bf16[32,16,768]{2,1,0:T(8,128)(2,1)} %broadcast_select_fusion.3), calls=%async_computation.1 | async-start | bytes 1572864 | tf_op jit(solution)/shard_map/all_to_all | solution.py:217
  135.8 27.2 %collective-permute-start.11 = (bf16[16,48,1536]{2,1,0:T(8,128)(2,1)}, bf16[16,48,1536]{2,1,0:T(8,128)(2,1)}, u32[]{:S(2)}, u32[]{:S(2)}) collective-permute-start(bf16[16,48,1536]{2,1,0:T(8,128)(2,1)} %constant_dynamic-update-slice_fusion.21.held), channel_id=1, source_target_pairs={{0,4},{4,0},{8,12},{12,8},{16,20},{20,16},{24,28},{28,24},{1,5},{5... | collective-permute-start | bytes 7077896 | tf_op jit(solution)/shard_map/ppermute | solution.py:248
  138.2 30.6 %collective-permute-start.17 = (bf16[16,192,384]{2,1,0:T(8,128)(2,1)}, bf16[16,192,384]{2,1,0:T(8,128)(2,1)}, u32[]{:S(2)}, u32[]{:S(2)}) collective-permute-start(bf16[16,192,384]{2,1,0:T(8,128)(2,1)} %constant_dynamic-update-slice_fusion.32.held), channel_id=1, source_target_pairs={{0,4},{4,0},{8,12},{12,8},{16,20},{20,16},{24,28},{28,24},{1,5},{5... | collective-permute-start | bytes 7077896 | tf_op jit(solution)/shard_map/ppermute | solution.py:248
  154.7 29.4 %collective-permute-start.5 = (bf16[16,208,384]{2,1,0:T(8,128)(2,1)}, bf16[16,208,384]{2,1,0:T(8,128)(2,1)}, u32[]{:S(2)}, u32[]{:S(2)}) collective-permute-start(bf16[16,208,384]{2,1,0:T(8,128)(2,1)} %constant_dynamic-update-slice_fusion.10.held), channel_id=1, source_target_pairs={{0,4},{4,0},{8,12},{12,8},{16,20},{20,16},{24,28},{28,24},{1,5},{5... | collective-permute-start | bytes 7667720 | tf_op jit(solution)/shard_map/ppermute | solution.py:248
  155.6 22.1 %all-to-all-start.4 = ((bf16[32,16,768]{2,1,0:T(8,128)(2,1)}), bf16[32,16,768]{2,1,0:T(8,128)(2,1)S(1)}, u32[]{:S(2)}, u32[]{:S(2)}) async-start(bf16[32,16,768]{2,1,0:T(8,128)(2,1)} %bitcast.22), calls=%async_computation.4 | async-start | bytes 1572864 | tf_op jit(solution)/shard_map/all_to_all | solution.py:215
  179.4 57.0 %all-to-all-start.5 = ((bf16[32,16,768]{2,1,0:T(8,128)(2,1)}), bf16[32,16,768]{2,1,0:T(8,128)(2,1)S(1)}, u32[]{:S(2)}, u32[]{:S(2)}) async-start(bf16[32,16,768]{2,1,0:T(8,128)(2,1)} %broadcast_select_fusion.2), calls=%async_computation.5 | async-start | bytes 1572864 | tf_op jit(solution)/shard_map/all_to_all | solution.py:217
  295.1 36.0 %collective-permute-start.18 = (bf16[768,1152]{1,0:T(8,128)(2,1)}, bf16[768,1152]{1,0:T(8,128)(2,1)}, u32[]{:S(2)}, u32[]{:S(2)}) collective-permute-start(bf16[768,1152]{1,0:T(8,128)(2,1)} %convolution_convert_fusion.2), channel_id=1, source_target_pairs={{0,4},{4,0},{8,12},{12,8},{16,20},{20,16},{24,28},{28,24},{1,5},{5... | collective-permute-start | bytes 5308424 | tf_op jit(solution)/shard_map/ppermute | solution.py:516
  299.2 36.8 %collective-permute-start.42 = (bf16[3072,384]{1,0:T(8,128)(2,1)}, bf16[3072,384]{1,0:T(8,128)(2,1)}, u32[]{:S(2)}, u32[]{:S(2)}) collective-permute-start(bf16[3072,384]{1,0:T(8,128)(2,1)} %convolution_convert_fusion), channel_id=1, source_target_pairs={{0,4},{4,0},{8,12},{12,8},{16,20},{20,16},{24,28},{28,24},{1,5},{5... | collective-permute-start | bytes 7077896 | tf_op jit(solution)/shard_map/ppermute | solution.py:516
  307.1 41.4 %collective-permute-start.32 = (bf16[768,1536]{1,0:T(8,128)(2,1)}, bf16[768,1536]{1,0:T(8,128)(2,1)}, u32[]{:S(2)}, u32[]{:S(2)}) collective-permute-start(bf16[768,1536]{1,0:T(8,128)(2,1)} %convolution_convert_fusion.1), channel_id=1, source_target_pairs={{0,4},{4,0},{8,12},{12,8},{16,20},{20,16},{24,28},{28,24},{1,5},{5... | collective-permute-start | bytes 7077896 | tf_op jit(solution)/shard_map/ppermute | solution.py:516
  319.0 24.5 %all-to-all-start.6 = ((bf16[32,16,768]{2,1,0:T(8,128)(2,1)}), bf16[32,16,768]{2,1,0:T(8,128)(2,1)S(1)}, u32[]{:S(2)}, u32[]{:S(2)}) async-start(bf16[32,16,768]{2,1,0:T(8,128)(2,1)} %bitcast.205), calls=%async_computation.6 | async-start | bytes 1572864 | tf_op jit(solution)/shard_map/all_to_all | solution.py:215
  327.2 44.0 %collective-permute-start.30 = (f32[72,128]{1,0:T(8,128)}, f32[72,128]{1,0:T(8,128)}, u32[]{:S(2)}, u32[]{:S(2)}) collective-permute-start(f32[72,128]{1,0:T(8,128)} %add.401), channel_id=1, source_target_pairs={{0,8},{1,9},{2,10},{3,11},{4,12},{5,13},{6,14},{7,15},{8,0},{9,1},... | collective-permute-start | bytes 110600 | tf_op jit(solution)/shard_map/ppermute | solution.py:572
  335.6 29.2 %collective-permute-start.19 = (bf16[4,96,1152]{2,1,0:T(8,128)(2,1)}, bf16[4,96,1152]{2,1,0:T(8,128)(2,1)}, u32[]{:S(2)}, u32[]{:S(2)}) collective-permute-start(bf16[4,96,1152]{2,1,0:T(8,128)(2,1)} %dynamic-slice_bitcast_fusion.2), channel_id=1, source_target_pairs={{0,8},{4,12},{8,0},{12,4},{16,24},{20,28},{24,16},{28,20},{1,9},{5... | collective-permute-start | bytes 2654216 | tf_op jit(solution)/shard_map/ppermute | solution.py:528
  341.8 65.7 %collective-permute-start.43 = (bf16[4,384,384]{2,1,0:T(8,128)(2,1)}, bf16[4,384,384]{2,1,0:T(8,128)(2,1)}, u32[]{:S(2)}, u32[]{:S(2)}) collective-permute-start(bf16[4,384,384]{2,1,0:T(8,128)(2,1)} %dynamic-slice_bitcast_fusion.1), channel_id=1, source_target_pairs={{0,8},{4,12},{8,0},{12,4},{16,24},{20,28},{24,16},{28,20},{1,9},{5... | collective-permute-start | bytes 3538952 | tf_op jit(solution)/shard_map/ppermute | solution.py:528
  343.5 50.1 %all-to-all-start.2 = ((bf16[32,16,768]{2,1,0:T(8,128)(2,1)}), bf16[32,16,768]{2,1,0:T(8,128)(2,1)}, u32[]{:S(2)}, u32[]{:S(2)}) async-start(bf16[32,16,768]{2,1,0:T(8,128)(2,1)} %bitcast.19), calls=%async_computation.2 | async-start | bytes 1572864 | tf_op jit(solution)/shard_map/all_to_all | solution.py:215
  367.9 34.6 %collective-permute-start.20 = (bf16[4,48,1152]{2,1,0:T(8,128)(2,1)}, bf16[4,48,1152]{2,1,0:T(8,128)(2,1)S(1)}, u32[]{:S(2)}, u32[]{:S(2)}) collective-permute-start(bf16[4,48,1152]{2,1,0:T(8,128)(2,1)} %dynamic-slice_bitcast_fusion.6), channel_id=1, source_target_pairs={{0,16},{4,20},{8,24},{12,28},{16,0},{20,4},{24,8},{28,12},{1,17},{... | collective-permute-start | bytes 1327112 | tf_op jit(solution)/shard_map/ppermute | solution.py:528
  370.6 49.8 %collective-permute-start.34 = (bf16[4,96,1920]{2,1,0:T(8,128)(2,1)}, bf16[4,96,1920]{2,1,0:T(8,128)(2,1)}, u32[]{:S(2)}, u32[]{:S(2)}) collective-permute-start(bf16[4,96,1920]{2,1,0:T(8,128)(2,1)} %dynamic-slice_bitcast_fusion), channel_id=1, source_target_pairs={{0,16},{4,20},{8,24},{12,28},{16,0},{20,4},{24,8},{28,12},{1,17},{... | collective-permute-start | bytes 4423688 | tf_op jit(solution)/shard_map/ppermute | solution.py:528
  372.0 123.1 %collective-permute-start.31 = (f32[72,128]{1,0:T(8,128)S(1)}, f32[72,128]{1,0:T(8,128)S(1)}, u32[]{:S(2)}, u32[]{:S(2)}) collective-permute-start(f32[72,128]{1,0:T(8,128)S(1)} %add.402), channel_id=1, source_target_pairs={{0,16},{1,17},{2,18},{3,19},{4,20},{5,21},{6,22},{7,23},{8,24},{9,... | collective-permute-start | bytes 110600 | tf_op jit(solution)/shard_map/ppermute | solution.py:572
  399.0 75.2 %all-to-all-start.7 = ((bf16[32,16,768]{2,1,0:T(8,128)(2,1)}), bf16[32,16,768]{2,1,0:T(8,128)(2,1)}, u32[]{:S(2)}, u32[]{:S(2)}) async-start(bf16[32,16,768]{2,1,0:T(8,128)(2,1)} %get-tuple-element.129), calls=%async_computation.7 | async-start | bytes 1572864 | tf_op jit(solution)/shard_map/all_to_all | solution.py:217
  407.5 24.9 %collective-permute-start.22 = (bf16[48,1152]{1,0:T(8,128)(2,1)S(1)}, bf16[48,1152]{1,0:T(8,128)(2,1)S(1)}, u32[]{:S(2)}, u32[]{:S(2)}) collective-permute-start(bf16[48,1152]{1,0:T(8,128)(2,1)S(1)} %get-tuple-element.90), channel_id=1, source_target_pairs={{0,2},{1,3},{2,0},{3,1},{4,6},{5,7},{6,4},{7,5},{8,10},{9,11},{10,... | collective-permute-start | bytes 331784 | tf_op jit(solution)/shard_map/ppermute | solution.py:539
  432.5 39.5 %collective-permute-start.24 = (bf16[1,48,1152]{2,1,0:T(8,128)(2,1)S(1)}, bf16[1,48,1152]{2,1,0:T(8,128)(2,1)S(1)}, u32[]{:S(2)}, u32[]{:S(2)}) collective-permute-start(bf16[1,48,1152]{2,1,0:T(8,128)(2,1)S(1)} %fusion.51), channel_id=1, source_target_pairs={{0,16},{4,20},{8,24},{12,28},{16,0},{20,4},{24,8},{28,12},{1,17},{... | collective-permute-start | bytes 331784 | tf_op jit(solution)/shard_map/ppermute | solution.py:247
  474.2 24.3 %all-to-all-start.3 = ((bf16[32,16,768]{2,1,0:T(8,128)(2,1)}), bf16[32,16,768]{2,1,0:T(8,128)(2,1)S(1)}, u32[]{:S(2)}, u32[]{:S(2)}) async-start(bf16[32,16,768]{2,1,0:T(8,128)(2,1)} %get-tuple-element.130), calls=%async_computation.3 | async-start | bytes 1572864 | tf_op jit(solution)/shard_map/all_to_all | solution.py:217
  (67 other events, 694.3 us)
